TPU v7x, 32 devices: a whole 2x2x4 slice. The times are simulated.
32 devices in a mesh: wall: 8 (over y, x, core), span: 4 (over z).
Axes of the slice: x: 2, y: 2, z: 4, core: 2. Of those that a mesh axis runs over, the one named last changes fastest.
Arguments:
- velocity_old: float32 [3, 128, 64, 128], P(None, 'wall', 'span'), may hold values from -12 to 12, as said below
- heights: float32 [16], replicated, may hold values from 0.04 to 0.25
- owner_device: int32 [16384, 1], P(('wall', 'span')), may hold values from 0 to 7, as said below
- owner_element: int32 [16384, 1], P(('wall', 'span')), may hold values from 0 to 63, as said below
- ref_coords: float32 [3, 16384], P(None, ('wall', 'span')), may hold values from -1 to 1
- roughness: float32 [16384], P(('wall', 'span')), may hold values from 0.0001 to 0.01
Outputs:
- velocity_new: float32 [3, 128, 64, 128], P(None, 'wall', 'span')
- neumann: float32 [2, 16384], P(None, ('wall', 'span'))
Inputs may be any that keep to these rules, and one draw needn't show every extreme that they name: `velocity_old`: values at coinciding nodes of neighbouring elements are equal. `owner_device`: the owner is the streamwise index w of the point's own device, or w + 1 or w - 1 modulo 8. Among the rows of one device at most 128 name w + 1 and at most 128 name w - 1; some device has exactly 128 for w + 1 and some device exactly 128 for w - 1. `owner_element`: the element index is (ex * 2 + ez) * 16 + ey with ex = i // 8 and ez = j // 8 of the wall point; ey < 2 for points of the first wall, ey >= 14 for the second.
All inputs are finite; a program needn't handle non-finite values.
Results may differ from a plain program's by a relative error of at most 0.0003.
Values sent between devices are 32-bit elements; how exact they have to be, the bound alone decides.
No kernel may reach another device: no remote copies, remote signals or barrier semaphores. Data moves between devices by JAX's collectives and lax.ppermute only.
A program may use at most 128 MiB of HBM per device.

v0:
```python
import math

import jax
import jax.numpy as jnp
import numpy as np
from jax import lax
from jax.sharding import PartitionSpec as P

ITERS = 3


GLL_NODES = (
    -1.0,
    -0.8717401485096066,
    -0.5917001814331423,
    -0.2092992179024789,
    0.2092992179024789,
    0.5917001814331423,
    0.8717401485096066,
    1.0,
)
GLL_WEIGHTS = (
    0.03571428571428571,
    0.2107042271435061,
    0.3411226924835044,
    0.4124587946587038,
    0.4124587946587038,
    0.3411226924835044,
    0.2107042271435061,
    0.03571428571428571,
)
viscosity = 0.02
inverse_step = 20.0
karman = 0.41
sample_height = 0.1
speed_floor = 0.01
element_dx = 0.05
element_dz = 0.13
precise = lax.Precision.HIGHEST


def with_halo(cells, sides, width):
    for axis, dim in sides:
        count = lax.axis_size(axis)
        head = lax.slice_in_dim(cells, 0, width, axis=dim)
        tail = lax.slice_in_dim(cells, cells.shape[dim] - width, cells.shape[dim], axis=dim)
        cells = jnp.concatenate(
            [
                lax.ppermute(tail, axis, [(i, (i + 1) % count) for i in range(count)]),
                cells,
                lax.ppermute(head, axis, [((i + 1) % count, i) for i in range(count)]),
            ],
            axis=dim,
        )
    return cells


def shifted(value, axis, steps):
    count = lax.axis_size(axis)
    pairs = [(source, (source + steps) % count) for source in range(count)]
    return lax.ppermute(value, axis, pairs)


def stiffness_table():
    points = np.array(GLL_NODES)
    weights = np.array(GLL_WEIGHTS)
    previous = np.ones(8)
    current = points.copy()
    for degree in range(1, 7):
        previous, current = (
            current,
            ((2 * degree + 1) * points * current - degree * previous) / (degree + 1),
        )
    derivative = np.zeros((8, 8))
    for target in range(8):
        for source in range(8):
            if target != source:
                derivative[target, source] = (
                    current[target] / current[source] / (points[target] - points[source])
                )
    derivative[0, 0] = -14.0
    derivative[7, 7] = 14.0
    return derivative.T @ (weights[:, None] * derivative)


def lagrange(coord):
    points = np.array(GLL_NODES)
    gaps_table = points[:, None] - points[None, :] + np.eye(8)
    scale_row = jnp.asarray(1.0 / np.prod(gaps_table, axis=1), jnp.float32)
    gaps = coord[:, None] - jnp.asarray(points, jnp.float32)[None, :]
    filled = jnp.where(jnp.asarray(np.eye(8) > 0.5)[None], jnp.float32(1.0), gaps[:, None, :])
    return jnp.prod(filled, axis=2) * scale_row[None, :]


def face_weights(length, open_ends):
    values = np.ones(length)
    position = np.arange(length) % 8
    values[(position == 0) | (position == 7)] = 0.5
    if open_ends:
        values[0] = 1.0
        values[-1] = 1.0
    return values


def join_faces(core, before, after, axis):
    count = core.shape[axis] // 8
    blocks = core.reshape(core.shape[:axis] + (count, 8) + core.shape[axis + 1 :])
    first = lax.slice_in_dim(blocks, 0, 1, axis=axis + 1)
    last = lax.slice_in_dim(blocks, 7, 8, axis=axis + 1)
    before_b = jnp.expand_dims(before, axis + 1)
    after_b = jnp.expand_dims(after, axis + 1)
    prev_last = jnp.concatenate([before_b, lax.slice_in_dim(last, 0, count - 1, axis=axis)], axis)
    next_first = jnp.concatenate([lax.slice_in_dim(first, 1, count, axis=axis), after_b], axis)
    middle = lax.slice_in_dim(blocks, 1, 7, axis=axis + 1)
    joined = jnp.concatenate([first + prev_last, middle, last + next_first], axis + 1)
    return joined.reshape(core.shape)


def assemble(local):
    padded = with_halo(local, (("wall", 1), ("span", 2)), 1)
    joined_x = join_faces(padded[:, 1:-1], padded[:, :1], padded[:, -1:], 1)
    joined_z = join_faces(joined_x[:, :, 1:-1], joined_x[:, :, :1], joined_x[:, :, -1:], 2)
    border = jnp.zeros(joined_z.shape[:3] + (1,), jnp.float32)
    return join_faces(joined_z, border, border, 3)


def paired_total(first, second):
    return lax.psum((first, second), ("wall", "span"))


def spread(values):
    return values[:, None, None, None]


def slot_numbers(selected, capacity):
    ranking = jnp.cumsum(selected.astype(jnp.int32)) - 1
    return jnp.where(selected, ranking, capacity)


def body(velocity_old, heights, owner_device, owner_element, ref_coords, roughness):
    weights = np.array(GLL_WEIGHTS)
    stiffness = stiffness_table()
    length_x, length_z, length_y = (
        velocity_old.shape[1],
        velocity_old.shape[2],
        velocity_old.shape[3],
    )
    count_x, count_z, count_y = (length_x // 8, length_z // 8, length_y // 8)
    stiff_x = jnp.asarray(np.kron(np.eye(count_x), stiffness * (2.0 / element_dx)), jnp.float32)
    stiff_z = jnp.asarray(np.kron(np.eye(count_z), stiffness * (2.0 / element_dz)), jnp.float32)
    blocks = (2.0 / heights)[:, None, None] * jnp.asarray(stiffness, jnp.float32)[None]
    stiff_y = jnp.einsum("ef,eab->eafb", jnp.eye(count_y, dtype=jnp.float32), blocks).reshape(
        length_y, length_y
    )
    mass_x = jnp.asarray(np.tile(0.5 * element_dx * weights, count_x), jnp.float32)
    mass_z = jnp.asarray(np.tile(0.5 * element_dz * weights, count_z), jnp.float32)
    mass_y = (0.5 * heights[:, None] * jnp.asarray(weights, jnp.float32)[None, :]).reshape(length_y)
    mass_xb = mass_x[None, :, None, None]
    mass_zb = mass_z[None, None, :, None]
    mass_yb = mass_y[None, None, None, :]
    mass_all = mass_xb * mass_zb * mass_yb
    inverse_count = jnp.asarray(
        face_weights(length_x, False)[:, None, None]
        * face_weights(length_z, False)[None, :, None]
        * face_weights(length_y, True)[None, None, :],
        jnp.float32,
    )

    def operate(field):
        along_x = jnp.einsum("ab,cbzy->cazy", stiff_x, field, precision=precise)
        along_z = jnp.einsum("ab,cxby->cxay", stiff_z, field, precision=precise)
        along_y = jnp.einsum("cxzb,ab->cxza", field, stiff_y, precision=precise)
        local = (
            viscosity
            * (
                along_x * mass_zb * mass_yb
                + mass_xb * along_z * mass_yb
                + mass_xb * mass_zb * along_y
            )
            + inverse_step * mass_all * field
        )
        return assemble(local)

    def weighted(first, second):
        return jnp.sum(first * second * inverse_count[None], axis=(1, 2, 3))

    element_rows = (
        velocity_old.reshape(3, count_x, 8, count_z, 8, count_y, 8)
        .transpose(1, 3, 5, 0, 2, 4, 6)
        .reshape(count_x * count_z * count_y, 3 * 512)
    )

    def interpolate(ids_in, coords_in):
        point_total = ids_in.shape[0]
        groups = math.gcd(point_total, 8)
        grouped_ids = ids_in.reshape(groups, point_total // groups)
        grouped_coords = coords_in.T.reshape(groups, point_total // groups, 3)

        def evaluate(pieces):
            row_ids, coords = pieces
            values = element_rows[row_ids].reshape(row_ids.shape[0], 3, 8, 8, 8)
            return jnp.einsum(
                "gcabd,ga,gb,gd->gc",
                values,
                lagrange(coords[:, 0]),
                lagrange(coords[:, 1]),
                lagrange(coords[:, 2]),
                precision=precise,
            )

        result = lax.map(evaluate, (grouped_ids, grouped_coords))
        return result.reshape(point_total, 3).T

    wall_count = lax.axis_size("wall")
    point_count = owner_device.shape[0]
    capacity = point_count // 4
    own_wall = lax.axis_index("wall")
    distance = (owner_device[:, 0] - own_wall + wall_count) % wall_count
    to_next = distance == 1
    to_prev = distance == wall_count - 1
    slot_next = slot_numbers(to_next, capacity)
    slot_prev = slot_numbers(to_prev, capacity)
    packed = jnp.concatenate([owner_element[:, 0].astype(jnp.float32)[None], ref_coords], axis=0)
    empty_buffer = jnp.zeros((4, capacity + 1), jnp.float32)
    send_next = empty_buffer.at[:, slot_next].set(packed)[:, :capacity]
    send_prev = empty_buffer.at[:, slot_prev].set(packed)[:, :capacity]
    got_next = shifted(send_next, "wall", 1)
    got_prev = shifted(send_prev, "wall", -1)
    answer_next = interpolate(got_next[0].astype(jnp.int32), got_next[1:])
    answer_prev = interpolate(got_prev[0].astype(jnp.int32), got_prev[1:])
    back_next = shifted(answer_next, "wall", -1)
    back_prev = shifted(answer_prev, "wall", 1)
    own_values = interpolate(owner_element[:, 0], ref_coords)
    zero_column = jnp.zeros((3, 1), jnp.float32)
    from_next = jnp.concatenate([back_next, zero_column], axis=1)[:, slot_next]
    from_prev = jnp.concatenate([back_prev, zero_column], axis=1)[:, slot_prev]
    velocity_pts = jnp.where(
        to_next[None], from_next, jnp.where(to_prev[None], from_prev, own_values)
    )
    stream = velocity_pts[0]
    spanwise = velocity_pts[2]
    wall_speed = jnp.sqrt(stream * stream + spanwise * spanwise + speed_floor)
    drag_coeff = (karman / jnp.log(sample_height / roughness)) ** 2
    neumann = -(drag_coeff * wall_speed / viscosity)[None, :] * jnp.stack([stream, spanwise])
    traction = (viscosity * neumann).reshape(2, 2, length_x, length_z) * (
        mass_x[:, None] * mass_z[None, :]
    )[None, None]
    zero_plane = jnp.zeros((1, length_x, length_z), jnp.float32)
    bottom = jnp.concatenate([traction[0:1, 0], zero_plane, traction[1:2, 0]], axis=0)
    top_wall = jnp.concatenate([traction[0:1, 1], zero_plane, traction[1:2, 1]], axis=0)
    forcing = inverse_step * mass_all * velocity_old
    forcing = forcing.at[:, :, :, 0].add(bottom).at[:, :, :, -1].add(top_wall)
    right_side = assemble(forcing)
    solution = jnp.zeros_like(right_side)
    residual = right_side
    applied = operate(residual)
    norm_now, product = paired_total(weighted(residual, residual), weighted(residual, applied))
    step_size = norm_now / product
    direction = residual
    along_dir = applied
    for sweep in range(ITERS):
        solution = solution + spread(step_size) * direction
        residual = residual - spread(step_size) * along_dir
        if sweep + 1 < ITERS:
            applied = operate(residual)
            norm_next, product = paired_total(
                weighted(residual, residual), weighted(residual, applied)
            )
            growth = norm_next / norm_now
            step_size = norm_next / (product - growth * norm_next / step_size)
            direction = residual + spread(growth) * direction
            along_dir = applied + spread(growth) * along_dir
            norm_now = norm_next
    return (solution, neumann)


def solution(mesh):
    placed = (
        P(None, "wall", "span", None),
        P(),
        P(("wall", "span"), None),
        P(("wall", "span"), None),
        P(None, ("wall", "span")),
        P(("wall", "span")),
    )
    return jax.shard_map(
        body,
        mesh=mesh,
        in_specs=placed,
        out_specs=(P(None, "wall", "span", None), P(None, ("wall", "span"))),
        check_vma=False,
    )
```

profile of v0, /device:TPU:0, one launch (start us, length us, event | category | flops | bytes accessed | tf_op | source)
XLA Modules:
  0.0 405.1 jit_solution(9068878765870258537)
XLA Ops:
  7.2 3.4 collective-permute-start.2
  15.4 5.9 %reshape.740 = f32[3,2,8,2,8,16,8]{6,5,4,3,2,1,0:T(8,128)} reshape(f32[3,16,16,128]{3,2,1,0:T(8,128)} %param.50) | data formatting | bytes 786432 | tf_op jit(solution)/shard_map/reshape | solution.py:188
  21.6 6.8 %copy.466 = f32[2,2,16,3,8,8,8]{2,1,0,6,5,4,3:T(2,128)} copy(f32[2,2,16,3,8,8,8]{6,2,5,1,4,0,3:T(8,128)} %bitcast.359) | data formatting | bytes 786432 | tf_op jit(solution)/shard_map/transpose | solution.py:189
  28.5 4.0 reshape.741
  32.7 18.7 %while.40 = (s32[]{:T(128)}, f32[8,64,3]{1,0,2:T(8,128)S(1)}, f32[8,64,3]{1,0,2:T(8,128)S(1)}, s32[8,64]{1,0:T(8,128)S(1)}, f32[64,1536]{1,0:T(8,128)S(1)}, /*in...) while((s32[]{:T(128)}, f32[8,64,3]{1,0,2:T(8,128)S(1)}, ...), condition=%wide.region_20.21_spmd.clone.clone, body=%wide.region_16.20_spmd.sunk.clone.clone.sunk | while | flops 229378 | bytes 2121465 | solution.py:211
  52.4 15.5 %while.39 = (s32[]{:T(128)}, f32[8,16,3]{1,2,0:T(4,128)S(1)}, f32[8,16,3]{1,2,0:T(4,128)S(1)}, s32[8,16]{1,0:T(8,128)S(1)}, f32[64,1536]{1,0:T(8,128)S(1)}, /*in...) while((s32[]{:T(128)}, f32[8,16,3]{1,2,0:T(4,128)S(1)}, ...), condition=%wide.region_15.16_spmd.clone.clone, body=%wide.region_11.15_spmd.sunk.clone.clone.sunk | while | flops 58114 | bytes 536561 | solution.py:211
  67.9 15.5 %while.38 = (s32[]{:T(128)}, f32[8,16,3]{1,2,0:T(4,128)S(1)}, f32[8,16,3]{1,2,0:T(4,128)S(1)}, s32[8,16]{1,0:T(8,128)S(1)}, f32[64,1536]{1,0:T(8,128)S(1)}, /*in...) while((s32[]{:T(128)}, f32[8,16,3]{1,2,0:T(4,128)S(1)}, ...), condition=%wide.region_7.8_spmd.clone.clone, body=%wide.region_3.7_spmd.sunk.clone.clone.sunk | while | flops 58114 | bytes 536561 | solution.py:211
  93.1 3.1 scatter-add.6
  96.4 6.2 %scatter-add.9 = f32[3,16,16,128]{3,1,2,0:T(8,128)S(1)} dynamic-update-slice(f32[3,16,16,128]{3,1,2,0:T(8,128)S(1)} %scatter-add.6, f32[3,16,16,1]{3,1,2,0:T(8,128)S(1)} %slice_add_fusion.8, s32[]{:T(128)} %constant.175.clone.1, s32[]{:T(128)} %constant.175.clone.1, s32[]{:T(128)} %constant.175.clone.1, s32[]{:T(128)} %constant.185.clone.1) | dynamic-update-slice | bytes 6148 | tf_op jit(solution)/shard_map/scatter-add | solution.py:252
  119.1 3.9 slice_add_fusion.7
  129.7 5.6 %copy.591 = f32[3,16,16,128]{2,3,1,0:T(8,128)} copy(f32[3,16,16,128]{1,3,2,0:T(8,128)} %fusion.52) | data formatting | bytes 786432 | tf_op jit(solution)/shard_map/reshape | solution.py:116
  135.4 7.0 %fusion.38 = f32[3,16,16,128]{3,2,1,0:T(8,128)S(1)} fusion(f32[3,16,16,128]{2,3,1,0:T(8,128)} %copy.591, f32[128,128,1,1]{1,0,2,3:T(8,128)} %reshape.854), kind=kOutput, calls=%fused_computation.161 | convolution fusion | flops 150994944 | bytes 851968 | tf_op jit(solution)/shard_map/cxzb,ab->cxza/dot_general | solution.py:172
  142.5 3.6 fusion.14
  146.1 4.1 %fusion.20 = f32[3,16,16,128]{3,1,2,0:T(8,128)S(1)} fusion(f32[16,16,1,1]{1,0,3,2:T(8,128)S(1)} %copy-done.32, f32[3,16,16,128]{3,2,1,0:T(8,128)S(1)} %fusion.38, f32[3,16,16,128]{3,2,1,0:T(8,128)S(1)} %fusion.14, f32[3,16,16,128]{3,1,2,0:T(8,128)S(1)} %copy-done.18, f32[128]{0:T(128)S(1)} %copy-done.34, f32[16]{0:T(128)S(1)} %copy-done.40, ...), kind=kOutput, calls=%fused_computation.101 | convolution fusion | flops 19857408 | bytes 2099776 | tf_op jit(solution)/shard_map/ab,cbzy->cazy/dot_general | solution.py:170
  161.9 3.2 copy.509
  165.2 3.2 fusion.56
  171.0 5.1 %slice_add_fusion.5 = (f32[3,16,16,16,1]{1,4,3,2,0:T(1,128)S(1)}, f32[3,16,16,16,1]{1,4,3,2,0:T(1,128)S(1)}) fusion(f32[3,16,16,16,8]{1,4,3,2,0:T(8,128)} %bitcast.365, f32[3,16,16,15,1]{1,4,3,2,0:T(1,128)S(1)} %get-tuple-element.616, f32[3,16,16,15,1]{1,4,3,2,0:T(1,128)S(1)} %get-tuple-element.617), kind=kLoop, calls=%fused_computation.121 | loop fusion | flops 24576 | bytes 288768 | tf_op jit(solution)/shard_map/add | solution.py:115
  176.1 4.2 %multiply_reduce_fusion.6 = (f32[3]{0:T(128)}, f32[3]{0:T(128)}) fusion(f32[16,16,16,8]{0,3,2,1:T(8,128)S(1)} %copy-done.13, f32[3,16,16,16,1]{1,4,3,2,0:T(1,128)S(1)} %get-tuple-element.615, f32[3,16,16,16,6]{1,4,3,2,0:T(8,128)S(1)} %slice.663, f32[3,16,16,16,1]{1,4,3,2,0:T(1,128)S(1)} %get-tuple-element.614, f32[3,16,16,16,1]{1,4,3,2,0:T(1,128)S(1)} %copy-done.10, ...), kind=kLoop, calls=%fused_computation.85 | loop fusion | flops 983034 | bytes 917528 | tf_op jit(solution)/shard_map/reduce_sum | solution.py:185
  180.4 39.5 %all-reduce.12 = (f32[3]{0:T(128)}, f32[3]{0:T(128)}) all-reduce(f32[3]{0:T(128)} %get-tuple-element.523, f32[3]{0:T(128)} %get-tuple-element.522), channel_id=1, replica_groups=mesh['wall'=8,'span'=4] {'wall','span'}, use_global_device_ids=true, to_apply=%region_22.23 | all-reduce | flops 6 | bytes 48 | tf_op jit(solution)/shard_map/psum | solution.py:128
  220.6 6.0 %multiply_subtract_fusion.1 = (f32[3,16,16,16,8]{1,4,3,2,0:T(8,128)}, f32[3,16,16,128]{1,3,2,0:T(8,128)}) fusion(f32[3]{0:T(128)S(1)} %div.49, f32[3,16,16,16,1]{1,4,3,2,0:T(1,128)} %copy-done.17, f32[3,16,16,16,6]{1,4,3,2,0:T(8,128)} %copy-done, f32[3,16,16,16,1]{1,4,3,2,0:T(1,128)} %copy-done.16, f32[3,16,16,16,1]{1,4,3,2,0:T(1,128)} %copy-done.8, ...), kind=kLoop, calls=%fused_computation.84 | loop fusion | flops 589824 | bytes 1572876 | tf_op jit(solution)/shard_map/sub | solution.py:263
  226.5 3.2 copy.512
  233.6 4.1 %copy.595 = f32[3,16,16,128]{2,3,1,0:T(8,128)} copy(f32[3,16,16,128]{1,3,2,0:T(8,128)S(1)} %bitcast.357) | data formatting | bytes 786432 | tf_op jit(solution)/shard_map/sub | solution.py:263
  237.7 7.0 %fusion.36 = f32[3,16,16,128]{3,2,1,0:T(8,128)S(1)} fusion(f32[3,16,16,128]{2,3,1,0:T(8,128)} %copy.595, f32[128,128,1,1]{1,0,2,3:T(8,128)} %reshape.854), kind=kOutput, calls=%fused_computation.159 | convolution fusion | flops 150994944 | bytes 851968 | tf_op jit(solution)/shard_map/cxzb,ab->cxza/dot_general | solution.py:172
  266.9 38.9 %all-reduce.11 = (f32[3]{0:T(128)}, f32[3]{0:T(128)}) all-reduce(f32[3]{0:T(128)} %get-tuple-element.527, f32[3]{0:T(128)} %get-tuple-element.526), channel_id=1, replica_groups=mesh['wall'=8,'span'=4] {'wall','span'}, use_global_device_ids=true, to_apply=%region_26.27 | all-reduce | flops 6 | bytes 48 | tf_op jit(solution)/shard_map/psum | solution.py:128
  307.1 6.7 %multiply_subtract_fusion = (f32[3,16,16,16,8]{1,4,3,2,0:T(8,128)}, f32[3,16,16,128]{1,3,2,0:T(8,128)}) fusion(f32[3,16,16,16,8]{1,4,3,2,0:T(8,128)} %get-tuple-element.604, f32[3]{0:T(128)S(1)} %get-tuple-element.570, f32[3]{0:T(128)S(1)} %get-tuple-element.568, f32[3,16,16,16,1]{1,4,3,2,0:T(1,128)} %copy-done.20, f32[3,16,16,16,6]{1,4,3,2,0:T(8,128)} %copy-done.6, ...), kind=kLoop, calls=%fused_computation.81 | loop fusion | flops 786432 | bytes 1966104 | tf_op jit(solution)/shard_map/sub | solution.py:263
  313.8 3.2 copy.533
  321.7 4.1 %copy.596 = f32[3,16,16,128]{2,3,1,0:T(8,128)} copy(f32[3,16,16,128]{1,3,2,0:T(8,128)S(1)} %bitcast.358) | data formatting | bytes 786432 | tf_op jit(solution)/shard_map/sub | solution.py:263
  325.8 7.0 %fusion.34 = f32[3,16,16,128]{3,2,1,0:T(8,128)S(1)} fusion(f32[3,16,16,128]{2,3,1,0:T(8,128)} %copy.596, f32[128,128,1,1]{1,0,2,3:T(8,128)} %reshape.854), kind=kOutput, calls=%fused_computation.157 | convolution fusion | flops 150994944 | bytes 851968 | tf_op jit(solution)/shard_map/cxzb,ab->cxza/dot_general | solution.py:172
  346.1 3.3 copy.549
  349.4 3.2 fusion.54
  354.9 3.9 slice_add_fusion.1
  362.0 39.9 %all-reduce.10 = (f32[3]{0:T(128)S(1)}, f32[3]{0:T(128)S(1)}) all-reduce(f32[3]{0:T(128)} %get-tuple-element.525, f32[3]{0:T(128)} %get-tuple-element.524), channel_id=1, replica_groups=mesh['wall'=8,'span'=4] {'wall','span'}, use_global_device_ids=true, to_apply=%region_30.31 | all-reduce | flops 6 | bytes 48 | tf_op jit(solution)/shard_map/psum | solution.py:128
  (792 shorter events, 161.4 us)
Async XLA Ops:
  7.2 44.4 %collective-permute-start.2 = (f32[4,128]{0,1:T(8,128)S(1)}, f32[4,128]{0,1:T(8,128)S(1)}, u32[]{:S(2)}, u32[]{:S(2)}) collective-permute-start(f32[4,128]{0,1:T(8,128)S(1)} %slice.614), channel_id=1, source_target_pairs={{0,28},{4,0},{8,4},{12,8},{16,12},{20,16},{24,20},{28,24},{1,29},{... | collective-permute-start | bytes 6152 | tf_op jit(solution)/shard_map/ppermute | solution.py:61
  12.9 39.0 %collective-permute-start = (f32[4,128]{0,1:T(8,128)S(1)}, f32[4,128]{0,1:T(8,128)S(1)}, u32[]{:S(2)}, u32[]{:S(2)}) collective-permute-start(f32[4,128]{0,1:T(8,128)S(1)} %slice.611), channel_id=1, source_target_pairs={{0,4},{4,8},{8,12},{12,16},{16,20},{20,24},{24,28},{28,0},{1,5},{5... | collective-permute-start | bytes 6152 | tf_op jit(solution)/shard_map/ppermute | solution.py:61
  32.7 18.7 %copy-start.51 = (f32[8,8]{1,0:T(8,128)S(1)}, f32[8,8]{1,0:T(8,128)}, u32[]{:S(2)}) copy-start(f32[8,8]{1,0:T(8,128)} %constant.189.clone) | copy-start | bytes 772
  67.9 23.6 %copy-start.52 = (f32[512]{0:T(512)S(1)}, f32[512]{0:T(512)}, u32[]{:S(2)}) copy-start(f32[512]{0:T(512)} %param.55) | copy-start | bytes 6148
  83.7 6.0 %collective-permute-start.3 = (f32[3,128]{0,1:T(8,128)S(1)}, f32[3,128]{0,1:T(8,128)S(1)}, u32[]{:S(2)}, u32[]{:S(2)}) collective-permute-start(f32[3,128]{0,1:T(8,128)S(1)} %bitcast.404), channel_id=1, source_target_pairs={{0,4},{4,8},{8,12},{12,16},{16,20},{20,24},{24,28},{28,0},{1,5},{5... | collective-permute-start | bytes 4616 | tf_op jit(solution)/shard_map/ppermute | solution.py:61
  83.7 4.8 %collective-permute-start.1 = (f32[3,128]{0,1:T(8,128)S(1)}, f32[3,128]{0,1:T(8,128)S(1)}, u32[]{:S(2)}, u32[]{:S(2)}) collective-permute-start(f32[3,128]{0,1:T(8,128)S(1)} %bitcast.405), channel_id=1, source_target_pairs={{0,28},{4,0},{8,4},{12,8},{16,12},{20,16},{24,20},{28,24},{1,29},{... | collective-permute-start | bytes 4616 | tf_op jit(solution)/shard_map/ppermute | solution.py:61
  102.6 4.3 %collective-permute-start.4 = (f32[3,1,16,128]{3,1,2,0:T(1,128)S(1)}, f32[3,1,16,128]{3,1,2,0:T(1,128)S(1)}, u32[]{:S(2)}, u32[]{:S(2)}) collective-permute-start(f32[3,1,16,128]{3,1,2,0:T(1,128)S(1)} %get-tuple-element.684), channel_id=1, source_target_pairs={{0,4},{4,8},{8,12},{12,16},{16,20},{20,24},{24,28},{28,0},{1,5},{5... | collective-permute-start | bytes 73736 | tf_op jit(solution)/shard_map/ppermute | solution.py:49
  102.7 4.3 %collective-permute-start.5 = (f32[3,1,16,128]{3,1,2,0:T(1,128)S(1)}, f32[3,1,16,128]{3,1,2,0:T(1,128)S(1)}, u32[]{:S(2)}, u32[]{:S(2)}) collective-permute-start(f32[3,1,16,128]{3,1,2,0:T(1,128)S(1)} %get-tuple-element.685), channel_id=1, source_target_pairs={{4,0},{8,4},{12,8},{16,12},{20,16},{24,20},{28,24},{0,28},{5,1},{9... | collective-permute-start | bytes 73736 | tf_op jit(solution)/shard_map/ppermute | solution.py:51
  107.0 5.9 %collective-permute-start.6 = (f32[3,18,1,128]{3,1,2,0:T(8,128)S(1)}, f32[3,18,1,128]{3,1,2,0:T(8,128)S(1)}, u32[]{:S(2)}, u32[]{:S(2)}) collective-permute-start(f32[3,18,1,128]{3,1,2,0:T(8,128)S(1)} %get-tuple-element.660), channel_id=1, source_target_pairs={{0,1},{1,2},{2,3},{3,0},{4,5},{5,6},{6,7},{7,4},{8,9},{9,10},{10,1... | collective-permute-start | bytes 82952 | tf_op jit(solution)/shard_map/ppermute | solution.py:49
  108.6 4.4 %collective-permute-start.7 = (f32[3,18,1,128]{3,1,2,0:T(8,128)S(1)}, f32[3,18,1,128]{3,1,2,0:T(8,128)S(1)}, u32[]{:S(2)}, u32[]{:S(2)}) collective-permute-start(f32[3,18,1,128]{3,1,2,0:T(8,128)S(1)} %get-tuple-element.661), channel_id=1, source_target_pairs={{1,0},{2,1},{3,2},{0,3},{5,4},{6,5},{7,6},{4,7},{9,8},{10,9},{11,1... | collective-permute-start | bytes 82952 | tf_op jit(solution)/shard_map/ppermute | solution.py:51
  135.3 10.7 %copy-start.9 = (f32[3,16,16,16,1]{1,4,3,2,0:T(1,128)S(1)}, f32[3,16,16,16,1]{1,4,3,2,0:T(1,128)}, u32[]{:S(2)}) copy-start(f32[3,16,16,16,1]{1,4,3,2,0:T(1,128)} %copy-done.8) | copy-start | bytes 147460
  135.4 10.7 %copy-start.18 = (f32[3,16,16,128]{3,1,2,0:T(8,128)S(1)}, f32[3,16,16,128]{3,1,2,0:T(8,128)}, u32[]{:S(2)}) copy-start(f32[3,16,16,128]{3,1,2,0:T(8,128)} %copy.492) | copy-start | bytes 1179652
  150.2 4.3 %collective-permute-start.8 = (f32[3,1,16,128]{3,1,2,0:T(1,128)S(1)}, f32[3,1,16,128]{3,1,2,0:T(1,128)S(1)}, u32[]{:S(2)}, u32[]{:S(2)}) collective-permute-start(f32[3,1,16,128]{3,1,2,0:T(1,128)S(1)} %get-tuple-element.678), channel_id=1, source_target_pairs={{0,4},{4,8},{8,12},{12,16},{16,20},{20,24},{24,28},{28,0},{1,5},{5... | collective-permute-start | bytes 73736 | tf_op jit(solution)/shard_map/ppermute | solution.py:49
  150.3 4.2 %collective-permute-start.9 = (f32[3,1,16,128]{3,1,2,0:T(1,128)S(1)}, f32[3,1,16,128]{3,1,2,0:T(1,128)S(1)}, u32[]{:S(2)}, u32[]{:S(2)}) collective-permute-start(f32[3,1,16,128]{3,1,2,0:T(1,128)S(1)} %get-tuple-element.679), channel_id=1, source_target_pairs={{4,0},{8,4},{12,8},{16,12},{20,16},{24,20},{28,24},{0,28},{5,1},{9... | collective-permute-start | bytes 73736 | tf_op jit(solution)/shard_map/ppermute | solution.py:51
  154.5 5.8 %collective-permute-start.10 = (f32[3,18,1,128]{3,1,2,0:T(8,128)S(1)}, f32[3,18,1,128]{3,1,2,0:T(8,128)S(1)}, u32[]{:S(2)}, u32[]{:S(2)}) collective-permute-start(f32[3,18,1,128]{3,1,2,0:T(8,128)S(1)} %get-tuple-element.652), channel_id=1, source_target_pairs={{0,1},{1,2},{2,3},{3,0},{4,5},{5,6},{6,7},{7,4},{8,9},{9,10},{10,1... | collective-permute-start | bytes 82952 | tf_op jit(solution)/shard_map/ppermute | solution.py:49
  155.7 4.6 %collective-permute-start.11 = (f32[3,18,1,128]{3,1,2,0:T(8,128)S(1)}, f32[3,18,1,128]{3,1,2,0:T(8,128)S(1)}, u32[]{:S(2)}, u32[]{:S(2)}) collective-permute-start(f32[3,18,1,128]{3,1,2,0:T(8,128)S(1)} %get-tuple-element.653), channel_id=1, source_target_pairs={{1,0},{2,1},{3,2},{0,3},{5,4},{6,5},{7,6},{4,7},{9,8},{10,9},{11,1... | collective-permute-start | bytes 82952 | tf_op jit(solution)/shard_map/ppermute | solution.py:51
  245.0 4.2 %collective-permute-start.12 = (f32[3,1,16,128]{3,1,2,0:T(1,128)S(1)}, f32[3,1,16,128]{3,1,2,0:T(1,128)S(1)}, u32[]{:S(2)}, u32[]{:S(2)}) collective-permute-start(f32[3,1,16,128]{3,1,2,0:T(1,128)S(1)} %get-tuple-element.672), channel_id=1, source_target_pairs={{0,4},{4,8},{8,12},{12,16},{16,20},{20,24},{24,28},{28,0},{1,5},{5... | collective-permute-start | bytes 73736 | tf_op jit(solution)/shard_map/ppermute | solution.py:49
  245.1 4.2 %collective-permute-start.13 = (f32[3,1,16,128]{3,1,2,0:T(1,128)S(1)}, f32[3,1,16,128]{3,1,2,0:T(1,128)S(1)}, u32[]{:S(2)}, u32[]{:S(2)}) collective-permute-start(f32[3,1,16,128]{3,1,2,0:T(1,128)S(1)} %get-tuple-element.673), channel_id=1, source_target_pairs={{4,0},{8,4},{12,8},{16,12},{20,16},{24,20},{28,24},{0,28},{5,1},{9... | collective-permute-start | bytes 73736 | tf_op jit(solution)/shard_map/ppermute | solution.py:51
  249.2 5.8 %collective-permute-start.14 = (f32[3,18,1,128]{3,1,2,0:T(8,128)S(1)}, f32[3,18,1,128]{3,1,2,0:T(8,128)S(1)}, u32[]{:S(2)}, u32[]{:S(2)}) collective-permute-start(f32[3,18,1,128]{3,1,2,0:T(8,128)S(1)} %get-tuple-element.644), channel_id=1, source_target_pairs={{0,1},{1,2},{2,3},{3,0},{4,5},{5,6},{6,7},{7,4},{8,9},{9,10},{10,1... | collective-permute-start | bytes 82952 | tf_op jit(solution)/shard_map/ppermute | solution.py:49
  251.2 5.0 %collective-permute-start.15 = (f32[3,18,1,128]{3,1,2,0:T(8,128)S(1)}, f32[3,18,1,128]{3,1,2,0:T(8,128)S(1)}, u32[]{:S(2)}, u32[]{:S(2)}) collective-permute-start(f32[3,18,1,128]{3,1,2,0:T(8,128)S(1)} %get-tuple-element.645), channel_id=1, source_target_pairs={{1,0},{2,1},{3,2},{0,3},{5,4},{6,5},{7,6},{4,7},{9,8},{10,9},{11,1... | collective-permute-start | bytes 82952 | tf_op jit(solution)/shard_map/ppermute | solution.py:51
  264.0 43.1 %copy-start.1 = (f32[3,16,16,16,6]{1,4,3,2,0:T(8,128)S(1)}, f32[3,16,16,16,6]{1,4,3,2,0:T(8,128)}, u32[]{:S(2)}) copy-start(f32[3,16,16,16,6]{1,4,3,2,0:T(8,128)} %copy-done) | copy-start | bytes 884740
  325.8 15.6 %copy-start.38 = (f32[512]{0:T(512)S(1)}, f32[512]{0:T(512)}, u32[]{:S(2)}) copy-start(f32[512]{0:T(512)} %copy-done.37) | copy-start | bytes 6148
  325.8 15.6 %copy-start.46 = (f32[1,512]{1,0:T(1,128)S(1)}, f32[1,512]{1,0:T(1,128)}, u32[]{:S(2)}) copy-start(f32[1,512]{1,0:T(1,128)} %get-tuple-element.690) | copy-start | bytes 6148
  325.8 15.6 %copy-start.47 = (f32[1,512]{1,0:T(1,128)S(1)}, f32[1,512]{1,0:T(1,128)}, u32[]{:S(2)}) copy-start(f32[1,512]{1,0:T(1,128)} %get-tuple-element.694) | copy-start | bytes 6148
  333.3 4.2 %collective-permute-start.16 = (f32[3,1,16,128]{3,1,2,0:T(1,128)S(1)}, f32[3,1,16,128]{3,1,2,0:T(1,128)S(1)}, u32[]{:S(2)}, u32[]{:S(2)}) collective-permute-start(f32[3,1,16,128]{3,1,2,0:T(1,128)S(1)} %get-tuple-element.666), channel_id=1, source_target_pairs={{0,4},{4,8},{8,12},{12,16},{16,20},{20,24},{24,28},{28,0},{1,5},{5... | collective-permute-start | bytes 73736 | tf_op jit(solution)/shard_map/ppermute | solution.py:49
  333.4 4.2 %collective-permute-start.17 = (f32[3,1,16,128]{3,1,2,0:T(1,128)S(1)}, f32[3,1,16,128]{3,1,2,0:T(1,128)S(1)}, u32[]{:S(2)}, u32[]{:S(2)}) collective-permute-start(f32[3,1,16,128]{3,1,2,0:T(1,128)S(1)} %get-tuple-element.667), channel_id=1, source_target_pairs={{4,0},{8,4},{12,8},{16,12},{20,16},{24,20},{28,24},{0,28},{5,1},{9... | collective-permute-start | bytes 73736 | tf_op jit(solution)/shard_map/ppermute | solution.py:51
  337.5 5.8 %collective-permute-start.18 = (f32[3,18,1,128]{3,1,2,0:T(8,128)S(1)}, f32[3,18,1,128]{3,1,2,0:T(8,128)S(1)}, u32[]{:S(2)}, u32[]{:S(2)}) collective-permute-start(f32[3,18,1,128]{3,1,2,0:T(8,128)S(1)} %get-tuple-element.636), channel_id=1, source_target_pairs={{0,1},{1,2},{2,3},{3,0},{4,5},{5,6},{6,7},{7,4},{8,9},{9,10},{10,1... | collective-permute-start | bytes 82952 | tf_op jit(solution)/shard_map/ppermute | solution.py:49
  339.6 4.8 %collective-permute-start.19 = (f32[3,18,1,128]{3,1,2,0:T(8,128)S(1)}, f32[3,18,1,128]{3,1,2,0:T(8,128)S(1)}, u32[]{:S(2)}, u32[]{:S(2)}) collective-permute-start(f32[3,18,1,128]{3,1,2,0:T(8,128)S(1)} %get-tuple-element.637), channel_id=1, source_target_pairs={{1,0},{2,1},{3,2},{0,3},{5,4},{6,5},{7,6},{4,7},{9,8},{10,9},{11,1... | collective-permute-start | bytes 82952 | tf_op jit(solution)/shard_map/ppermute | solution.py:51
  358.9 42.9 %copy-start.53 = (f32[3]{0:T(128)S(1)}, f32[3]{0:T(128)}, u32[]{:S(2)}) copy-start(f32[3]{0:T(128)} %get-tuple-element.562) | copy-start | bytes 40
  358.9 43.6 %copy-start.43 = (f32[3]{0:T(128)S(1)}, f32[3]{0:T(128)}, u32[]{:S(2)}) copy-start(f32[3]{0:T(128)} %copy-done.42) | copy-start | bytes 40
  358.9 43.6 %copy-start.45 = (f32[3]{0:T(128)S(1)}, f32[3]{0:T(128)}, u32[]{:S(2)}) copy-start(f32[3]{0:T(128)} %copy-done.44) | copy-start | bytes 40
  358.9 43.6 %copy-start.50 = (f32[3]{0:T(128)S(1)}, f32[3]{0:T(128)}, u32[]{:S(2)}) copy-start(f32[3]{0:T(128)} %copy-done.49) | copy-start | bytes 40
  (42 other events, 253.7 us)
where the time goes:
time: 413 us; the launch traced here: 405 us
  local copies, waits for them, and re-layouts  126 us (31%)
  blocking collectives  118 us (29%)
  other arithmetic  73.3 us (18%)
  matrix products  33.8 us (8%)
  starting transfers between devices  32.8 us (8%)
  waiting for transfers between devices  16.1 us (4%)
    psum x3, blocking collectives, paired_total(): return lax.psum((first, second), ('wall', 'span'))  118 us
    dot_general x3, matrix products, operate(): along_y = jnp.einsum('cxzb,ab->cxza', field, stiff_y, precision=precise)  21 us
    ppermute x8, starting transfers between devices, with_halo(): lax.ppermute(head, axis, [((i + 1) % count, i) for i in range(count)])  19.2 us
    gather x24, local copies, waits for them, and re-layouts, evaluate(): values = element_rows[row_ids].reshape(row_ids.shape[0], 3, 8, 8, 8)  15.4 us
    sub x4, other arithmetic, body(): residual = residual - spread(step_size) * along_dir  15.1 us
    reshape x4, local copies, waits for them, and re-layouts, join_faces(): return joined.reshape(core.shape)  15 us
    add x12, other arithmetic, join_faces(): first + prev_last  14.2 us
    while x96, local copies, waits for them, and re-layouts  12.7 us
  transfers between devices with their start and end apart: 20, of which 13 were waited for; matrix products, arithmetic and copies ran while one was open for 11% of the time, Pallas kernels for 0%

commit v1 on v0

v1 whole, which is shorter than its diff:
```python
import jax
import jax.numpy as jnp
import numpy as np
from jax import lax
from jax.experimental import pallas as pl
from jax.experimental.pallas import tpu as pltpu
from jax.sharding import PartitionSpec as P

NEAR = 2


GLL_NODES = (
    -1.0,
    -0.8717401485096066,
    -0.5917001814331423,
    -0.2092992179024789,
    0.2092992179024789,
    0.5917001814331423,
    0.8717401485096066,
    1.0,
)
GLL_WEIGHTS = (
    0.03571428571428571,
    0.2107042271435061,
    0.3411226924835044,
    0.4124587946587038,
    0.4124587946587038,
    0.3411226924835044,
    0.2107042271435061,
    0.03571428571428571,
)
viscosity = 0.02
inverse_step = 20.0
karman = 0.41
sample_height = 0.1
speed_floor = 0.01
element_dx = 0.05
element_dz = 0.13
precise = lax.Precision.HIGHEST


def shifted(value, axis, steps):
    count = lax.axis_size(axis)
    pairs = [(source, (source + steps) % count) for source in range(count)]
    return lax.ppermute(value, axis, pairs)


def stiffness_table():
    points = np.array(GLL_NODES)
    weights = np.array(GLL_WEIGHTS)
    previous = np.ones(8)
    current = points.copy()
    for degree in range(1, 7):
        previous, current = (
            current,
            ((2 * degree + 1) * points * current - degree * previous) / (degree + 1),
        )
    derivative = np.zeros((8, 8))
    for target in range(8):
        for source in range(8):
            if target != source:
                derivative[target, source] = (
                    current[target] / current[source] / (points[target] - points[source])
                )
    derivative[0, 0] = -14.0
    derivative[7, 7] = 14.0
    return derivative.T @ (weights[:, None] * derivative)


def face_weights(length, open_ends):
    values = np.ones(length)
    position = np.arange(length) % 8
    values[(position == 0) | (position == 7)] = 0.5
    if open_ends:
        values[0] = 1.0
        values[-1] = 1.0
    return values


def join_matrix(length):
    table = np.eye(length)
    for node in range(7, length - 1, 8):
        table[node, node + 1] = 1.0
        table[node + 1, node] = 1.0
    return table


def exchange(x_low, x_high, z_low, z_high):
    from_prev = shifted(x_high, "wall", 1)
    from_next = shifted(x_low, "wall", -1)

    def with_corners(face, spot):
        first = face[:, :1] + from_prev[:, spot]
        last = face[:, -1:] + from_next[:, spot]
        return jnp.concatenate([first, face[:, 1:-1], last], axis=1)

    z_low = with_corners(z_low, slice(0, 1))
    z_high = with_corners(z_high, slice(-1, None))
    return from_prev, from_next, shifted(z_high, "span", 1), shifted(z_low, "span", -1)


def call(kernel, outs, *operands):
    space = pl.BlockSpec(memory_space=pltpu.VMEM)
    return pl.pallas_call(
        kernel,
        out_shape=[jax.ShapeDtypeStruct(shape, jnp.float32) for shape in outs],
        in_specs=[space] * len(operands),
        out_specs=[space] * len(outs),
    )(*operands)


def dot(first, second):
    return jnp.dot(first, second, precision=precise, preferred_element_type=jnp.float32)


def body(velocity_old, heights, owner_device, owner_element, ref_coords, roughness):
    weights = np.array(GLL_WEIGHTS)
    points = np.array(GLL_NODES)
    stiffness = stiffness_table()
    _, length_x, length_z, length_y = velocity_old.shape
    count_x, count_z, count_y = (length_x // 8, length_z // 8, length_y // 8)
    plane = length_x * length_z
    point_total = owner_device.shape[0]
    near = NEAR * 8

    mass_x = np.tile(0.5 * element_dx * weights, count_x)
    mass_z = np.tile(0.5 * element_dz * weights, count_z)
    stiff_x = np.kron(np.eye(count_x), stiffness * (2.0 / element_dx))
    stiff_z = np.kron(np.eye(count_z), stiffness * (2.0 / element_dz))
    join_x, join_z, join_y = (join_matrix(n) for n in (length_x, length_z, length_y))
    join_xz = np.kron(join_x, join_z)
    mass_xz = np.kron(mass_x, mass_z)
    plane_op = viscosity * (
        np.kron(stiff_x, np.diag(mass_z)) + np.kron(np.diag(mass_x), stiff_z)
    )
    left = jnp.asarray(
        np.concatenate([join_xz @ np.diag(mass_xz), join_xz @ plane_op], axis=1), jnp.float32
    )
    tiled = np.tile(weights, count_y)
    stiff_part = np.concatenate(
        [
            2.0 * viscosity * np.kron(np.eye(count_y), stiffness) @ join_y,
            np.zeros((length_y, length_y)),
        ],
        axis=1,
    ).reshape(count_y, 8, 2 * length_y)
    mass_part = np.concatenate(
        [inverse_step * 0.5 * tiled[:, None] * join_y, 0.5 * tiled[:, None] * join_y], axis=1
    ).reshape(count_y, 8, 2 * length_y)
    tall = heights[:, None, None]
    right = (
        jnp.asarray(stiff_part, jnp.float32) / tall + jnp.asarray(mass_part, jnp.float32) * tall
    ).reshape(length_y, 2 * length_y)

    def edge_sum(values):
        position = np.arange(values.shape[0]) % 8
        return np.where((position == 0) | (position == 7), 2.0 * values, values)

    columns = np.zeros((plane, 8))
    columns[:, 0] = np.kron(face_weights(length_x, False), face_weights(length_z, False))
    columns[:, 1] = np.kron(face_weights(length_x, True), face_weights(length_z, True))
    columns[:, 2] = inverse_step * np.kron(edge_sum(mass_x), edge_sum(mass_z))
    columns = jnp.asarray(columns, jnp.float32)
    share_y = jnp.asarray(face_weights(length_y, True)[None, :], jnp.float32)

    def packed_near():
        pieces = []
        for ex in range(count_x):
            for comp in (0, 2):
                block = velocity_old[comp, ex * 8 : ex * 8 + 8]
                pieces.append(block[:, :, :near])
                pieces.append(block[:, :, length_y - near :])
        return jnp.concatenate(pieces, axis=2).reshape(8 * length_z, count_x * 4 * near)

    own_near = packed_near()
    prev_near = shifted(own_near, "wall", 1)
    next_near = shifted(own_near, "wall", -1)
    wall_count = lax.axis_size("wall")
    own_wall = lax.axis_index("wall")
    distance = ((owner_device[:, 0] - own_wall + wall_count) % wall_count)[None, :]
    relation = jnp.where(distance == 1, 1.0, jnp.where(distance == 0, 0.0, -1.0))
    layer = (owner_element[:, 0] % count_y)[None, :]
    layer = jnp.where(layer < NEAR, layer, layer - (count_y - NEAR)).astype(jnp.float32)
    per_point = jnp.concatenate([ref_coords, relation, layer, roughness[None, :]], axis=0)
    lanes = count_x * 4 * near
    scale = 1.0 / np.prod(points[:, None] - points[None, :] + np.eye(8), axis=1)
    mass_row = jnp.asarray(mass_xz[None, :], jnp.float32)
    pick_z = np.zeros((plane, 2 * length_x))
    for x in range(length_x):
        pick_z[x * length_z, x] = 1.0
        pick_z[x * length_z + length_z - 1, length_x + x] = 1.0
    pick_z = jnp.asarray(pick_z, jnp.float32)
    join_const = jnp.asarray(join_xz, jnp.float32)

    def sample_kernel(own, prev, nxt, info, mass, join, pick, neu, trac, xl, xh, zl, zh):
        def basis(row):
            coord = info[row : row + 1, :]
            gaps = [coord - np.float32(p) for p in points]
            rows = []
            for a in range(8):
                value = None
                for b in range(8):
                    if b != a:
                        value = gaps[b] if value is None else value * gaps[b]
                rows.append(value * np.float32(scale[a]))
            return jnp.concatenate(rows, axis=0)

        along_x, along_z, along_y = basis(0), basis(1), basis(2)
        relation_row, layer_row = info[3:4, :], info[4:5, :]
        near_y = jnp.concatenate(
            [jnp.where(layer_row == np.float32(e), along_y, 0.0) for e in range(NEAR)], axis=0
        )
        full_y = jnp.concatenate([near_y] * (lanes // near), axis=0)
        row = lax.broadcasted_iota(jnp.int32, (lanes, point_total), 0)
        col = lax.broadcasted_iota(jnp.int32, (lanes, point_total), 1)
        fits = (row // (4 * near) == col % plane // (8 * length_z)) & (
            row // near % 2 == col // plane
        )
        comp = row // (2 * near) % 2
        zrow = lax.broadcasted_iota(jnp.int32, (8 * length_z, point_total), 0)
        zcol = lax.broadcasted_iota(jnp.int32, (8 * length_z, point_total), 1)
        tall_z = jnp.concatenate([along_z] * (count_z * 8), axis=0)
        tall_x = jnp.concatenate(
            [jnp.broadcast_to(along_x[a : a + 1, :], (length_z, point_total)) for a in range(8)],
            axis=0,
        )
        mix = jnp.where(zrow % length_z // 8 == zcol % length_z // 8, tall_z * tall_x, 0.0)
        sampled = []
        for k in range(2):
            table = jnp.where(fits & (comp == k), full_y, 0.0)
            picked = jnp.where(
                relation_row == 0.0,
                dot(own[...], table),
                jnp.where(relation_row > 0.0, dot(nxt[...], table), dot(prev[...], table)),
            )
            sampled.append(jnp.sum(picked * mix, axis=0, keepdims=True))
        stream, spanwise = sampled
        speed = jnp.sqrt(stream * stream + spanwise * spanwise + speed_floor)
        ratio = karman / jnp.log(sample_height / info[5:6, :])
        factor = -(ratio * ratio * speed / viscosity)
        neu[0:1, :] = factor * stream
        neu[1:2, :] = factor * spanwise
        half = []
        for value in (stream, spanwise):
            for side in range(2):
                part = (viscosity * (factor * value))[:, side * plane : (side + 1) * plane]
                half.append(part * mass[...])
        stacked = jnp.concatenate(half, axis=0)
        joined = dot(stacked, join[...])
        trac[...] = joined
        xl[...] = joined[:, :length_z]
        xh[...] = joined[:, plane - length_z :]
        picked_z = dot(joined, pick[...])
        zl[...] = picked_z[:, :length_x]
        zh[...] = picked_z[:, length_x:]

    neumann, traction, *edges = call(
        sample_kernel,
        [(2, point_total), (4, plane), (4, length_z), (4, length_z), (4, length_x), (4, length_x)],
        own_near, prev_near, next_near, per_point, mass_row, join_const, pick_z,
    )
    around = exchange(*edges)

    shape = (3, length_x, length_z, length_y)
    x_face, z_face = (3, length_z, length_y), (3, length_x, length_y)
    outs = [shape, shape, x_face, x_face, z_face, z_face, (8, length_y)]

    def apply(comp, field, left_ref, right_ref, cols, share, sums):
        both = dot(field, right_ref[...])
        stacked = jnp.concatenate([both[:, :length_y], both[:, length_y:]], axis=0)
        applied = dot(left_ref[...], stacked)
        sums[comp : comp + 1, :] = share[...] * jnp.sum(
            field * field * cols[:, 0:1], axis=0, keepdims=True
        )
        sums[comp + 3 : comp + 4, :] = share[...] * jnp.sum(
            field * applied * cols[:, 1:2], axis=0, keepdims=True
        )
        return applied

    def store(comp, field, applied, u, t, xl, xh, zl, zh):
        u[comp] = field.reshape(length_x, length_z, length_y)
        cube = applied.reshape(length_x, length_z, length_y)
        t[comp] = cube
        xl[comp] = cube[0]
        xh[comp] = cube[length_x - 1]
        zl[comp] = cube[:, 0, :]
        zh[comp] = cube[:, length_z - 1, :]

    spread_pick = np.zeros((2 * length_z + 2 * length_x, plane))
    for z in range(length_z):
        spread_pick[z, z] = 1.0
        spread_pick[length_z + z, plane - length_z + z] = 1.0
    for x in range(length_x):
        spread_pick[2 * length_z + x, x * length_z] = 1.0
        spread_pick[2 * length_z + length_x + x, x * length_z + length_z - 1] = 1.0
    spread_pick = jnp.asarray(spread_pick, jnp.float32)

    def first_kernel(
        v, trac, xp, xn, zp, zn, place, left_ref, right_ref, cols, share,
        u, t, xl, xh, zl, zh, sums,
    ):
        edge = jnp.concatenate([xp[...], xn[...], zp[...], zn[...]], axis=1)
        wall = trac[...] + dot(edge, place[...])
        wall = jnp.concatenate([wall, jnp.zeros((4, plane), jnp.float32)], axis=0)
        wall = jnp.transpose(wall)
        lane = lax.broadcasted_iota(jnp.int32, (plane, length_y), 1)
        tall_y = jnp.sum(right_ref[:, length_y:], axis=0, keepdims=True)
        sums[...] = jnp.zeros((8, length_y), jnp.float32)
        for comp in range(3):
            field = v[comp].reshape(plane, length_y) * (cols[:, 2:3] * tall_y)
            if comp != 1:
                at = comp
                field = field + jnp.where(lane == 0, wall[:, at : at + 1], 0.0)
                field = field + jnp.where(
                    lane == length_y - 1, wall[:, at + 1 : at + 2], 0.0
                )
            applied = apply(comp, field, left_ref, right_ref, cols, share, sums)
            store(comp, field, applied, u, t, xl, xh, zl, zh)

    def add_faces(comp, t_in, xp, xn, zp, zn):
        cube = t_in[comp]
        ix = lax.broadcasted_iota(jnp.int32, cube.shape, 0)
        iz = lax.broadcasted_iota(jnp.int32, cube.shape, 1)
        cube = cube + jnp.where(ix == 0, xp[comp][None], 0.0)
        cube = cube + jnp.where(ix == length_x - 1, xn[comp][None], 0.0)
        cube = cube + jnp.where(iz == 0, zp[comp][:, None, :], 0.0)
        cube = cube + jnp.where(iz == length_z - 1, zn[comp][:, None, :], 0.0)
        return cube.reshape(plane, length_y)

    def next_kernel(
        t_in, xp, xn, zp, zn, left_ref, right_ref, cols, share, u, t, xl, xh, zl, zh, sums
    ):
        sums[...] = jnp.zeros((8, length_y), jnp.float32)
        for comp in range(3):
            field = add_faces(comp, t_in, xp, xn, zp, zn)
            applied = apply(comp, field, left_ref, right_ref, cols, share, sums)
            store(comp, field, applied, u, t, xl, xh, zl, zh)

    devices = wall_count * lax.axis_size("span")

    def last_kernel(
        t_in, xp, xn, zp, zn, left_ref, right_ref, cols, share, sums_0, sums_1, u, moments, sums
    ):
        sums[...] = jnp.zeros((8, length_y), jnp.float32)
        for comp in range(3):
            field = add_faces(comp, t_in, xp, xn, zp, zn)
            apply(comp, field, left_ref, right_ref, cols, share, sums)
            u[comp] = field.reshape(length_x, length_z, length_y)
        stacked = jnp.concatenate([sums_0[...], sums_1[...], sums[...]], axis=0)
        total = jnp.sum(stacked, axis=1, keepdims=True)
        row = lax.broadcasted_iota(jnp.int32, (24, 18), 0)
        col = lax.broadcasted_iota(jnp.int32, (24, 18), 1)
        chosen = (row % 8 < 6) & (row // 8 * 6 + row % 8 == col)
        line = jnp.sum(jnp.where(chosen, total, 0.0), axis=0, keepdims=True)
        moments[...] = jnp.broadcast_to(line, (devices, 18))

    def combine_kernel(moments, u0, u1, u2, out):
        line = jnp.sum(moments[...], axis=0, keepdims=True)
        mu = [line[:, 3 * k : 3 * k + 3] for k in range(6)]

        def gram(poly, offset):
            value = None
            for i, first in enumerate(poly):
                for j, second in enumerate(poly):
                    term = first * second * mu[i + j + offset]
                    value = term if value is None else value + term
            return value

        one = jnp.ones((1, 3), jnp.float32)
        zero = jnp.zeros((1, 3), jnp.float32)
        residual, direction, answer = [one], [one], [zero, zero, zero]
        norm_now = mu[0]
        for sweep in range(3):
            step = norm_now / gram(direction, 1)
            for i, value in enumerate(direction):
                answer[i] = answer[i] + step * value
            if sweep < 2:
                residual = residual + [zero]
                residual = [residual[0]] + [
                    residual[i + 1] - step * value for i, value in enumerate(direction)
                ]
                norm_next = gram(residual, 0)
                growth = norm_next / norm_now
                direction = [
                    value + growth * direction[i] if i < len(direction) else value
                    for i, value in enumerate(residual)
                ]
                norm_now = norm_next
        for comp in range(3):
            coef = [value[:, comp : comp + 1] for value in answer]
            out[comp] = (
                (coef[0] * u0[comp].reshape(plane, length_y))
                + (coef[1] * u1[comp].reshape(plane, length_y))
                + (coef[2] * u2[comp].reshape(plane, length_y))
            ).reshape(length_x, length_z, length_y)

    tables = (left, right, columns, share_y)
    u0, t0, *faces, sums_0 = call(
        first_kernel, outs, velocity_old, traction, *around, spread_pick, *tables
    )
    u1, t1, *faces, sums_1 = call(next_kernel, outs, t0, *exchange(*faces), *tables)
    u2, moments, _ = call(
        last_kernel, [shape, (devices, 18), (8, length_y)],
        t1, *exchange(*faces), *tables, sums_0, sums_1,
    )
    moments = lax.all_to_all(moments, ("wall", "span"), 0, 0, tiled=True)
    (answer,) = call(combine_kernel, [shape], moments, u0, u1, u2)
    return (answer, neumann)


def solution(mesh):
    placed = (
        P(None, "wall", "span", None),
        P(),
        P(("wall", "span"), None),
        P(("wall", "span"), None),
        P(None, ("wall", "span")),
        P(("wall", "span")),
    )
    return jax.shard_map(
        body,
        mesh=mesh,
        in_specs=placed,
        out_specs=(P(None, "wall", "span", None), P(None, ("wall", "span"))),
        check_vma=False,
    )
```

time: 413 us -> 81.2 us (0.20); the launches traced: 405 us -> 80.5 us
  local copies, waits for them, and re-layouts: 126 us -> 8.36 us
  blocking collectives: 118 us -> 10.4 us
  other arithmetic: 73.3 us -> 3.13 us
  matrix products: 33.8 us -> 0 us
  Pallas kernels: 0 us -> 21.7 us
  starting transfers between devices: 32.8 us -> 18.8 us
    psum x3 -> x0, blocking collectives: 118 us -> none  [paired_total(): return lax.psum((first, second), ('wall', 'span'))]
    dot_general x9 -> x0, matrix products: 33.8 us -> none  [the longest x3 21 us: operate(): along_y = jnp.einsum('cxzb,ab->cxza', field, stiff_y, precision=precise)]
    reshape x13 -> x0, local copies, waits for them, and re-layouts: 26.9 us -> none  [the longest x4 15 us: join_faces(): return joined.reshape(core.shape)]
    ppermute x16 -> x0, starting transfers between devices: 26.4 us -> none  [the longest x8 19.2 us: with_halo(): lax.ppermute(head, axis, [((i + 1) % count, i) for i in range(count)])]
    pallas_call x0 -> x5, Pallas kernels: none -> 21.7 us  [call(): pl.pallas_call(kernel, out_shape=[jax.ShapeDtypeStruct(shape, jnp.float32...]
    gather x28 -> x0, local copies, waits for them, and re-layouts: 17.6 us -> none  [the longest x24 15.4 us: evaluate(): values = element_rows[row_ids].reshape(row_ids.shape[0], 3, 8, 8, 8)]
    sub x30 -> x0, other arithmetic: 17 us -> none  [the longest x4 15.1 us: body(): residual = residual - spread(step_size) * along_dir]
    add x21 -> x3, other arithmetic: 17.4 us -> 1.55 us  [with_corners(): first = face[:, :1] + from_prev[:, spot]]
  transfers between devices with their start and end apart: 20 -> 14, of which waited for: 13 -> 10; matrix products, arithmetic and copies ran while one was open for 11% -> 4% of each run, Pallas kernels for 0% -> 0%
where the time goes in v1:
time: 81.2 us; the launch traced here: 80.5 us
  Pallas kernels  21.7 us (27%)
  starting transfers between devices  18.8 us (23%)
  waiting for transfers between devices  17.2 us (21%)
  blocking collectives  10.4 us (13%)
  local copies, waits for them, and re-layouts  8.36 us (10%)
  other arithmetic  3.13 us (4%)
  between operations  0.87 us (1%)
    pallas_call x5, Pallas kernels, call(): pl.pallas_call(kernel, out_shape=[jax.ShapeDtypeStruct(shape, jnp.float32...  21.7 us
    ppermute x14, starting transfers between devices, shifted(): return lax.ppermute(value, axis, pairs)  18.8 us
    ppermute x14, waiting for transfers between devices, shifted(): return lax.ppermute(value, axis, pairs)  17.2 us
    all_to_all x1, blocking collectives, body(): moments = lax.all_to_all(moments, ('wall', 'span'), 0, 0, tiled=True)  10.4 us
    unnamed x54, local copies, waits for them, and re-layouts  5.38 us
    slice x6, local copies, waits for them, and re-layouts, with_corners(): return jnp.concatenate([first, face[:, 1:-1], last], axis=1)  1.65 us
  transfers between devices with their start and end apart: 14, of which 10 were waited for; matrix products, arithmetic and copies ran while one was open for 4% of the time, Pallas kernels for 0%

profile of v1, /device:TPU:0, one launch (start us, length us, event | category | flops | bytes accessed | tf_op | source)
XLA Modules:
  0.0 80.5 jit_solution(8926411191619190246)
XLA Ops:
  0.6 1.0 %slice_bitcast_fusion = (f32[8,16,128]{2,1,0:T(8,128)S(1)}, f32[8,16,128]{2,1,0:T(8,128)S(1)}, f32[8,16,128]{2,1,0:T(8,128)S(1)}, f32[8,16,128]{2,1,0:T(8,128)S(1)}) fusion(f32[3,16,16,128]{3,2,1,0:T(8,128)} %v.1), kind=kLoop, calls=%fused_computation.2 | loop fusion | bytes 524288 | tf_op jit(solution)/shard_map/squeeze | solution.py:170
  2.0 3.4 %collective-permute-start.1 = (f32[128,128]{1,0:T(8,128)S(1)}, f32[128,128]{1,0:T(8,128)S(1)}, u32[]{:S(2)}, u32[]{:S(2)}) collective-permute-start(f32[128,128]{1,0:T(8,128)S(1)} %bitcast.20), channel_id=1, source_target_pairs={{0,28},{4,0},{8,4},{12,8},{16,12},{20,16},{24,20},{28,24},{1,29},{... | collective-permute-start | bytes 196616 | tf_op jit(solution)/shard_map/ppermute | solution.py:45
  5.5 0.6 copy-done.19
  6.2 0.6 pad_maximum_fusion.4.info
  7.4 2.7 %collective-permute-done.prev = f32[128,128]{1,0:T(8,128)S(1)} collective-permute-done((f32[128,128]{1,0:T(8,128)S(1)}, f32[128,128]{1,0:T(8,128)S(1)}, u32[]{:S(2)}, u32[]{:S(2)}) %collective-permute-start) | collective-permute-done | bytes 65568 | tf_op jit(solution)/shard_map/ppermute | solution.py:45
  10.0 0.6 copy-done.4
  10.7 3.8 %shard_map.158 = (f32[2,512]{1,0:T(2,128)}, f32[4,256]{1,0:T(4,128)}, f32[4,16]{1,0:T(4,128)}, f32[4,16]{1,0:T(4,128)}, f32[4,16]{1,0:T(4,128)}, /*index=5*/f32[4,16]{1,0:T(4,128)}) custom-call(f32[128,128]{1,0:T(8,128)} %bitcast.22, f32[128,128]{1,0:T(8,128)} %copy-done.4, f32[128,128]{1,0:T(8,128)} %copy-done.3, f32[6,512]{1,0:T(8,128)} %pad_maximum_fusion.4.info, ...), custom_call_target="tpu_custom_call" | custom-call | tf_op jit(solution)/shard_map/pallas_call | solution.py:104
  15.1 2.0 %collective-permute-start.3 = (f32[4,16]{1,0:T(4,128)S(1)}, f32[4,16]{1,0:T(4,128)S(1)}, u32[]{:S(2)}, u32[]{:S(2)}) collective-permute-start(f32[4,16]{1,0:T(4,128)S(1)} %copy-done.26), channel_id=1, source_target_pairs={{0,28},{4,0},{8,4},{12,8},{16,12},{20,16},{24,20},{28,24},{1,29},{... | collective-permute-start | bytes 776 | tf_op jit(solution)/shard_map/ppermute | solution.py:45
  17.9 0.7 collective-permute-done.2.xp
  19.3 3.6 %collective-permute-start.5 = (f32[4,16]{1,0:T(4,128)S(1)}, f32[4,16]{1,0:T(4,128)S(1)}, u32[]{:S(2)}, u32[]{:S(2)}) collective-permute-start(f32[4,16]{1,0:T(4,128)S(1)} %pad_maximum_fusion.6), channel_id=1, source_target_pairs={{0,3},{1,0},{2,1},{3,2},{4,7},{5,4},{6,5},{7,6},{8,11},{9,8},{10,9... | collective-permute-start | bytes 776 | tf_op jit(solution)/shard_map/ppermute | solution.py:45
  23.6 0.7 fusion.right_ref
  24.3 4.1 %collective-permute-done.4.zp = f32[4,16]{1,0:T(4,128)S(1)} collective-permute-done((f32[4,16]{1,0:T(4,128)S(1)}, f32[4,16]{1,0:T(4,128)S(1)}, u32[]{:S(2)}, u32[]{:S(2)}) %collective-permute-start.4) | collective-permute-done | bytes 288 | tf_op jit(solution)/shard_map/ppermute | solution.py:45
  29.0 5.1 %shard_map.159 = (f32[3,16,16,128]{3,2,1,0:T(8,128)}, f32[3,16,16,128]{3,2,1,0:T(8,128)}, f32[3,16,128]{2,1,0:T(8,128)}, f32[3,16,128]{2,1,0:T(8,128)}, f32[3,16...) custom-call(f32[3,16,16,128]{3,2,1,0:T(8,128)} %v.1, f32[4,256]{1,0:T(4,128)} %get-tuple-element.24.trac, ...), custom_call_target="tpu_custom_call" | custom-call | tf_op jit(solution)/shard_map/pallas_call | solution.py:104
  34.1 2.6 %collective-permute-start.7 = (f32[3,16,128]{2,1,0:T(8,128)}, f32[3,16,128]{2,1,0:T(8,128)S(1)}, u32[]{:S(2)}, u32[]{:S(2)}) collective-permute-start(f32[3,16,128]{2,1,0:T(8,128)} %get-tuple-element.31), channel_id=1, source_target_pairs={{0,28},{4,0},{8,4},{12,8},{16,12},{20,16},{24,20},{28,24},{1,29},{... | collective-permute-start | bytes 73736 | tf_op jit(solution)/shard_map/ppermute | solution.py:45
  36.7 0.7 slice.150
  37.5 1.0 %collective-permute-done.6.xp = f32[3,16,128]{2,1,0:T(8,128)S(1)} collective-permute-done((f32[3,16,128]{2,1,0:T(8,128)}, f32[3,16,128]{2,1,0:T(8,128)S(1)}, u32[]{:S(2)}, u32[]{:S(2)}) %collective-permute-start.6) | collective-permute-done | bytes 24608 | tf_op jit(solution)/shard_map/ppermute | solution.py:45
  38.5 0.7 slice_add_fusion.9
  39.3 2.1 %collective-permute-start.8 = (f32[3,16,128]{2,1,0:T(8,128)S(1)}, f32[3,16,128]{2,1,0:T(8,128)S(1)}, u32[]{:S(2)}, u32[]{:S(2)}) collective-permute-start(f32[3,16,128]{2,1,0:T(8,128)S(1)} %pad_maximum_fusion), channel_id=1, source_target_pairs={{0,1},{1,2},{2,3},{3,0},{4,5},{5,6},{6,7},{7,4},{8,9},{9,10},{10,1... | collective-permute-start | bytes 73736 | tf_op jit(solution)/shard_map/ppermute | solution.py:45
  41.4 1.7 %collective-permute-done.9.zn = f32[3,16,128]{2,1,0:T(8,128)S(1)} collective-permute-done((f32[3,16,128]{2,1,0:T(8,128)S(1)}, f32[3,16,128]{2,1,0:T(8,128)S(1)}, u32[]{:S(2)}, u32[]{:S(2)}) %collective-permute-start.9) | collective-permute-done | bytes 24608 | tf_op jit(solution)/shard_map/ppermute | solution.py:45
  43.1 1.9 %collective-permute-done.8.zp = f32[3,16,128]{2,1,0:T(8,128)S(1)} collective-permute-done((f32[3,16,128]{2,1,0:T(8,128)S(1)}, f32[3,16,128]{2,1,0:T(8,128)S(1)}, u32[]{:S(2)}, u32[]{:S(2)}) %collective-permute-start.8) | collective-permute-done | bytes 24608 | tf_op jit(solution)/shard_map/ppermute | solution.py:45
  45.0 0.6 copy-done.14
  45.6 5.3 %shard_map.160 = (f32[3,16,16,128]{3,2,1,0:T(8,128)}, f32[3,16,16,128]{3,2,1,0:T(8,128)}, f32[3,16,128]{2,1,0:T(8,128)}, f32[3,16,128]{2,1,0:T(8,128)}, f32[3,16...) custom-call(f32[3,16,16,128]{3,2,1,0:T(8,128)} %get-tuple-element.29.t_in, f32[3,16,128]{2,1,0:T(8,128)} %copy-done.8, ...), custom_call_target="tpu_custom_call" | custom-call | tf_op jit(solution)/shard_map/pallas_call | solution.py:104
  50.9 2.6 %collective-permute-start.11 = (f32[3,16,128]{2,1,0:T(8,128)}, f32[3,16,128]{2,1,0:T(8,128)S(1)}, u32[]{:S(2)}, u32[]{:S(2)}) collective-permute-start(f32[3,16,128]{2,1,0:T(8,128)} %get-tuple-element.36), channel_id=1, source_target_pairs={{0,28},{4,0},{8,4},{12,8},{16,12},{20,16},{24,20},{28,24},{1,29},{... | collective-permute-start | bytes 73736 | tf_op jit(solution)/shard_map/ppermute | solution.py:45
  53.6 0.7 slice.160
  54.3 1.0 %collective-permute-done.10.xp = f32[3,16,128]{2,1,0:T(8,128)S(1)} collective-permute-done((f32[3,16,128]{2,1,0:T(8,128)}, f32[3,16,128]{2,1,0:T(8,128)S(1)}, u32[]{:S(2)}, u32[]{:S(2)}) %collective-permute-start.10) | collective-permute-done | bytes 24608 | tf_op jit(solution)/shard_map/ppermute | solution.py:45
  55.3 0.7 slice_add_fusion.5
  56.2 2.2 %collective-permute-start.12 = (f32[3,16,128]{2,1,0:T(8,128)S(1)}, f32[3,16,128]{2,1,0:T(8,128)S(1)}, u32[]{:S(2)}, u32[]{:S(2)}) collective-permute-start(f32[3,16,128]{2,1,0:T(8,128)S(1)} %pad_maximum_fusion.2), channel_id=1, source_target_pairs={{0,1},{1,2},{2,3},{3,0},{4,5},{5,6},{6,7},{7,4},{8,9},{9,10},{10,1... | collective-permute-start | bytes 73736 | tf_op jit(solution)/shard_map/ppermute | solution.py:45
  58.4 1.6 %collective-permute-done.13.zn = f32[3,16,128]{2,1,0:T(8,128)S(1)} collective-permute-done((f32[3,16,128]{2,1,0:T(8,128)S(1)}, f32[3,16,128]{2,1,0:T(8,128)S(1)}, u32[]{:S(2)}, u32[]{:S(2)}) %collective-permute-start.13) | collective-permute-done | bytes 24608 | tf_op jit(solution)/shard_map/ppermute | solution.py:45
  60.0 2.1 %collective-permute-done.12.zp = f32[3,16,128]{2,1,0:T(8,128)S(1)} collective-permute-done((f32[3,16,128]{2,1,0:T(8,128)S(1)}, f32[3,16,128]{2,1,0:T(8,128)S(1)}, u32[]{:S(2)}, u32[]{:S(2)}) %collective-permute-start.12) | collective-permute-done | bytes 24608 | tf_op jit(solution)/shard_map/ppermute | solution.py:45
  62.6 5.2 %shard_map.161 = (f32[3,16,16,128]{3,2,1,0:T(8,128)}, f32[32,18]{1,0:T(8,128)}, f32[8,128]{1,0:T(8,128)}) custom-call(f32[3,16,16,128]{3,2,1,0:T(8,128)} %get-tuple-element.34.t_in, f32[3,16,128]{2,1,0:T(8,128)} %copy-done.7, f32[3,16,128]{2,1,0:T(8,128)} %copy-done.9, f32[3,16,128]{2,1,0:T(8,128)} %copy-done.13, f32[3,16,128]{2,1,0:T(8,128)} %copy-done.11, ...), custom_call_target="tpu_custom_call" | custom-call | tf_op jit(solution)/shard_map/pallas_call | solution.py:104
  67.8 10.4 %all_to_all.11 = f32[32,1,18]{2,1,0:T(1,128)} all-to-all(f32[32,1,18]{2,1,0:T(1,128)} %bitcast.24), channel_id=1, replica_groups=mesh['wall'=8,'span'=4] {'wall','span'}, dimensions={0} | all-to-all | bytes 4608 | tf_op jit(solution)/shard_map/all_to_all | solution.py:406
  78.2 2.3 %shard_map.162 = f32[3,16,16,128]{3,2,1,0:T(8,128)} custom-call(f32[32,18]{1,0:T(8,128)} %bitcast.23, f32[3,16,16,128]{3,2,1,0:T(8,128)} %get-tuple-element.42.u0, f32[3,16,16,128]{3,2,1,0:T(8,128)} %get-tuple-element.43.u1, f32[3,16,16,128]{3,2,1,0:T(8,128)} %get-tuple-element.44.u2), custom_call_target="tpu_custom_call" | custom-call | tf_op jit(solution)/shard_map/pallas_call | solution.py:104
  (79 shorter events, 5.1 us)
Async XLA Ops:
  1.8 3.7 %copy-start.22 = (s32[512,1]{0,1:T(1,128)S(1)}, s32[512,1]{0,1:T(1,128)}, u32[]{:S(2)}) copy-start(s32[512,1]{0,1:T(1,128)} %param.18) | copy-start | bytes 6148
  1.8 3.7 %copy-start.23 = (s32[512,1]{0,1:T(1,128)S(1)}, s32[512,1]{0,1:T(1,128)}, u32[]{:S(2)}) copy-start(s32[512,1]{0,1:T(1,128)} %param.17) | copy-start | bytes 6148
  1.8 3.7 %copy-start.24 = (f32[512]{0:T(512)S(1)}, f32[512]{0:T(512)}, u32[]{:S(2)}) copy-start(f32[512]{0:T(512)} %param.20) | copy-start | bytes 6148
  2.0 8.0 %copy-start = (f32[8,16,128]{2,1,0:T(8,128)}, f32[8,16,128]{2,1,0:T(8,128)S(1)}, u32[]{:S(2)}) copy-start(f32[8,16,128]{2,1,0:T(8,128)S(1)} %concatenate.24) | copy-start | bytes 196612
  2.0 5.3 %collective-permute-start.1 = (f32[128,128]{1,0:T(8,128)S(1)}, f32[128,128]{1,0:T(8,128)S(1)}, u32[]{:S(2)}, u32[]{:S(2)}) collective-permute-start(f32[128,128]{1,0:T(8,128)S(1)} %bitcast.20), channel_id=1, source_target_pairs={{0,28},{4,0},{8,4},{12,8},{16,12},{20,16},{24,20},{28,24},{1,29},{... | collective-permute-start | bytes 196616 | tf_op jit(solution)/shard_map/ppermute | solution.py:45
  5.5 4.6 %collective-permute-start = (f32[128,128]{1,0:T(8,128)S(1)}, f32[128,128]{1,0:T(8,128)S(1)}, u32[]{:S(2)}, u32[]{:S(2)}) collective-permute-start(f32[128,128]{1,0:T(8,128)S(1)} %bitcast.21), channel_id=1, source_target_pairs={{0,4},{4,8},{8,12},{12,16},{16,20},{20,24},{24,28},{28,0},{1,5},{5... | collective-permute-start | bytes 196616 | tf_op jit(solution)/shard_map/ppermute | solution.py:45
  5.5 0.7 copy-start.19
  7.4 2.7 %copy-start.3 = (f32[128,128]{1,0:T(8,128)}, f32[128,128]{1,0:T(8,128)S(1)}, u32[]{:S(2)}) copy-start(f32[128,128]{1,0:T(8,128)S(1)} %collective-permute-done.1.nxt) | copy-start | bytes 196612
  10.7 12.3 %copy-start.1 = (f32[16,8,256]{2,1,0:T(8,128)S(1)}, f32[16,8,256]{2,1,0:T(8,128)}, u32[]{:S(2)}) copy-start(f32[16,8,256]{2,1,0:T(8,128)} %constant.67.clone) | copy-start | bytes 393220
  10.7 12.3 %copy-start.2 = (f32[16,8,256]{2,1,0:T(8,128)S(1)}, f32[16,8,256]{2,1,0:T(8,128)}, u32[]{:S(2)}) copy-start(f32[16,8,256]{2,1,0:T(8,128)} %constant.66.clone) | copy-start | bytes 393220
  14.5 2.7 %copy-start.18 = (f32[4,16]{1,0:T(4,128)S(1)}, f32[4,16]{1,0:T(4,128)}, u32[]{:S(2)}) copy-start(f32[4,16]{1,0:T(4,128)} %get-tuple-element.27) | copy-start | bytes 772
  14.5 4.2 %collective-permute-start.2 = (f32[4,16]{1,0:T(4,128)}, f32[4,16]{1,0:T(4,128)S(1)}, u32[]{:S(2)}, u32[]{:S(2)}) collective-permute-start(f32[4,16]{1,0:T(4,128)} %get-tuple-element.25), channel_id=1, source_target_pairs={{0,4},{4,8},{8,12},{12,16},{16,20},{20,24},{24,28},{28,0},{1,5},{5... | collective-permute-start | bytes 776 | tf_op jit(solution)/shard_map/ppermute | solution.py:45
  15.1 3.5 %collective-permute-start.3 = (f32[4,16]{1,0:T(4,128)S(1)}, f32[4,16]{1,0:T(4,128)S(1)}, u32[]{:S(2)}, u32[]{:S(2)}) collective-permute-start(f32[4,16]{1,0:T(4,128)S(1)} %copy-done.26), channel_id=1, source_target_pairs={{0,28},{4,0},{8,4},{12,8},{16,12},{20,16},{24,20},{28,24},{1,29},{... | collective-permute-start | bytes 776 | tf_op jit(solution)/shard_map/ppermute | solution.py:45
  19.3 5.0 %collective-permute-start.5 = (f32[4,16]{1,0:T(4,128)S(1)}, f32[4,16]{1,0:T(4,128)S(1)}, u32[]{:S(2)}, u32[]{:S(2)}) collective-permute-start(f32[4,16]{1,0:T(4,128)S(1)} %pad_maximum_fusion.6), channel_id=1, source_target_pairs={{0,3},{1,0},{2,1},{3,2},{4,7},{5,4},{6,5},{7,6},{8,11},{9,8},{10,9... | collective-permute-start | bytes 776 | tf_op jit(solution)/shard_map/ppermute | solution.py:45
  23.0 5.4 %collective-permute-start.4 = (f32[4,16]{1,0:T(4,128)S(1)}, f32[4,16]{1,0:T(4,128)S(1)}, u32[]{:S(2)}, u32[]{:S(2)}) collective-permute-start(f32[4,16]{1,0:T(4,128)S(1)} %pad_maximum_fusion.5), channel_id=1, source_target_pairs={{0,1},{1,2},{2,3},{3,0},{4,5},{5,6},{6,7},{7,4},{8,9},{9,10},{10,1... | collective-permute-start | bytes 776 | tf_op jit(solution)/shard_map/ppermute | solution.py:45
  24.3 4.1 %copy-start.20 = (f32[4,16]{1,0:T(4,128)}, f32[4,16]{1,0:T(4,128)S(1)}, u32[]{:S(2)}) copy-start(f32[4,16]{1,0:T(4,128)S(1)} %collective-permute-done.5.zn) | copy-start | bytes 772
  34.1 4.4 %collective-permute-start.6 = (f32[3,16,128]{2,1,0:T(8,128)}, f32[3,16,128]{2,1,0:T(8,128)S(1)}, u32[]{:S(2)}, u32[]{:S(2)}) collective-permute-start(f32[3,16,128]{2,1,0:T(8,128)} %get-tuple-element.30), channel_id=1, source_target_pairs={{0,4},{4,8},{8,12},{12,16},{16,20},{20,24},{24,28},{28,0},{1,5},{5... | collective-permute-start | bytes 73736 | tf_op jit(solution)/shard_map/ppermute | solution.py:45
  34.1 4.4 %collective-permute-start.7 = (f32[3,16,128]{2,1,0:T(8,128)}, f32[3,16,128]{2,1,0:T(8,128)S(1)}, u32[]{:S(2)}, u32[]{:S(2)}) collective-permute-start(f32[3,16,128]{2,1,0:T(8,128)} %get-tuple-element.31), channel_id=1, source_target_pairs={{0,28},{4,0},{8,4},{12,8},{16,12},{20,16},{24,20},{28,24},{1,29},{... | collective-permute-start | bytes 73736 | tf_op jit(solution)/shard_map/ppermute | solution.py:45
  36.7 0.8 copy-start.5
  38.5 0.8 copy-start.8
  38.5 0.8 copy-start.10
  39.3 3.9 %collective-permute-start.9 = (f32[3,16,128]{2,1,0:T(8,128)S(1)}, f32[3,16,128]{2,1,0:T(8,128)S(1)}, u32[]{:S(2)}, u32[]{:S(2)}) collective-permute-start(f32[3,16,128]{2,1,0:T(8,128)S(1)} %pad_maximum_fusion.1), channel_id=1, source_target_pairs={{0,3},{1,0},{2,1},{3,2},{4,7},{5,4},{6,5},{7,6},{8,11},{9,8},{10,9... | collective-permute-start | bytes 73736 | tf_op jit(solution)/shard_map/ppermute | solution.py:45
  39.3 5.7 %collective-permute-start.8 = (f32[3,16,128]{2,1,0:T(8,128)S(1)}, f32[3,16,128]{2,1,0:T(8,128)S(1)}, u32[]{:S(2)}, u32[]{:S(2)}) collective-permute-start(f32[3,16,128]{2,1,0:T(8,128)S(1)} %pad_maximum_fusion), channel_id=1, source_target_pairs={{0,1},{1,2},{2,3},{3,0},{4,5},{5,6},{6,7},{7,4},{8,9},{9,10},{10,1... | collective-permute-start | bytes 73736 | tf_op jit(solution)/shard_map/ppermute | solution.py:45
  43.1 1.9 %copy-start.12 = (f32[3,16,128]{2,1,0:T(8,128)}, f32[3,16,128]{2,1,0:T(8,128)S(1)}, u32[]{:S(2)}) copy-start(f32[3,16,128]{2,1,0:T(8,128)S(1)} %collective-permute-done.9.zn) | copy-start | bytes 73732
  50.9 4.4 %collective-permute-start.10 = (f32[3,16,128]{2,1,0:T(8,128)}, f32[3,16,128]{2,1,0:T(8,128)S(1)}, u32[]{:S(2)}, u32[]{:S(2)}) collective-permute-start(f32[3,16,128]{2,1,0:T(8,128)} %get-tuple-element.35), channel_id=1, source_target_pairs={{0,4},{4,8},{8,12},{12,16},{16,20},{20,24},{24,28},{28,0},{1,5},{5... | collective-permute-start | bytes 73736 | tf_op jit(solution)/shard_map/ppermute | solution.py:45
  50.9 4.4 %collective-permute-start.11 = (f32[3,16,128]{2,1,0:T(8,128)}, f32[3,16,128]{2,1,0:T(8,128)S(1)}, u32[]{:S(2)}, u32[]{:S(2)}) collective-permute-start(f32[3,16,128]{2,1,0:T(8,128)} %get-tuple-element.36), channel_id=1, source_target_pairs={{0,28},{4,0},{8,4},{12,8},{16,12},{20,16},{24,20},{28,24},{1,29},{... | collective-permute-start | bytes 73736 | tf_op jit(solution)/shard_map/ppermute | solution.py:45
  53.6 0.8 copy-start.6
  55.3 0.8 copy-start.7
  55.3 0.8 copy-start.9
  56.1 3.9 %collective-permute-start.13 = (f32[3,16,128]{2,1,0:T(8,128)S(1)}, f32[3,16,128]{2,1,0:T(8,128)S(1)}, u32[]{:S(2)}, u32[]{:S(2)}) collective-permute-start(f32[3,16,128]{2,1,0:T(8,128)S(1)} %pad_maximum_fusion.3), channel_id=1, source_target_pairs={{0,3},{1,0},{2,1},{3,2},{4,7},{5,4},{6,5},{7,6},{8,11},{9,8},{10,9... | collective-permute-start | bytes 73736 | tf_op jit(solution)/shard_map/ppermute | solution.py:45
  56.2 5.9 %collective-permute-start.12 = (f32[3,16,128]{2,1,0:T(8,128)S(1)}, f32[3,16,128]{2,1,0:T(8,128)S(1)}, u32[]{:S(2)}, u32[]{:S(2)}) collective-permute-start(f32[3,16,128]{2,1,0:T(8,128)S(1)} %pad_maximum_fusion.2), channel_id=1, source_target_pairs={{0,1},{1,2},{2,3},{3,0},{4,5},{5,6},{6,7},{7,4},{8,9},{9,10},{10,1... | collective-permute-start | bytes 73736 | tf_op jit(solution)/shard_map/ppermute | solution.py:45
  60.0 2.1 %copy-start.11 = (f32[3,16,128]{2,1,0:T(8,128)}, f32[3,16,128]{2,1,0:T(8,128)S(1)}, u32[]{:S(2)}) copy-start(f32[3,16,128]{2,1,0:T(8,128)S(1)} %collective-permute-done.13.zn) | copy-start | bytes 73732
  (9 other events, 5.6 us)

commit v2 on v1

--- a/solution.py
+++ b/solution.py
@@ -185,14 +185,7 @@
     lanes = count_x * 4 * near
     scale = 1.0 / np.prod(points[:, None] - points[None, :] + np.eye(8), axis=1)
     mass_row = jnp.asarray(mass_xz[None, :], jnp.float32)
-    pick_z = np.zeros((plane, 2 * length_x))
-    for x in range(length_x):
-        pick_z[x * length_z, x] = 1.0
-        pick_z[x * length_z + length_z - 1, length_x + x] = 1.0
-    pick_z = jnp.asarray(pick_z, jnp.float32)
-    join_const = jnp.asarray(join_xz, jnp.float32)
-
-    def sample_kernel(own, prev, nxt, info, mass, join, pick, neu, trac, xl, xh, zl, zh):
+    def sample_kernel(own, prev, nxt, info, mass, neu, trac):
         def basis(row):
             coord = info[row : row + 1, :]
             gaps = [coord - np.float32(p) for p in points]
@@ -245,40 +238,55 @@
             for side in range(2):
                 part = (viscosity * (factor * value))[:, side * plane : (side + 1) * plane]
                 half.append(part * mass[...])
-        stacked = jnp.concatenate(half, axis=0)
-        joined = dot(stacked, join[...])
-        trac[...] = joined
-        xl[...] = joined[:, :length_z]
-        xh[...] = joined[:, plane - length_z :]
-        picked_z = dot(joined, pick[...])
-        zl[...] = picked_z[:, :length_x]
-        zh[...] = picked_z[:, length_x:]
-
-    neumann, traction, *edges = call(
+        trac[...] = jnp.concatenate(half, axis=0)
+
+    neumann, traction = call(
         sample_kernel,
-        [(2, point_total), (4, plane), (4, length_z), (4, length_z), (4, length_x), (4, length_x)],
-        own_near, prev_near, next_near, per_point, mass_row, join_const, pick_z,
-    )
-    around = exchange(*edges)
+        [(2, point_total), (4, plane)],
+        own_near, prev_near, next_near, per_point, mass_row,
+    )
+
+    def plane_tables(length, mass, stiff):
+        join = join_matrix(3 * length)
+        wide_mass = join @ np.diag(np.tile(mass, 3)) @ join
+        wide_stiff = join @ np.kron(np.eye(3), stiff) @ join
+        return np.stack([join, wide_mass, wide_stiff])[:, length : 2 * length]
+
+    ops_x = jnp.asarray(plane_tables(length_x, mass_x, stiff_x), jnp.float32)
+    ops_z = jnp.asarray(plane_tables(length_z, mass_z, stiff_z), jnp.float32)
+    wide = jnp.concatenate(
+        [shifted(traction, "wall", 1), traction, shifted(traction, "wall", -1)], axis=1
+    ).reshape(4, 3 * length_x, length_z)
+    along = jnp.einsum("oxs,csz->ocxz", ops_x, wide, precision=precise)
+    wide = jnp.concatenate(
+        [shifted(along, "span", 1), along, shifted(along, "span", -1)], axis=3
+    )
+    both = jnp.einsum("ocxs,pzs->opcxz", wide, ops_z, precision=precise)
+    walls = jnp.concatenate(
+        [both[0, 0], both[1, 1], viscosity * (both[2, 1] + both[1, 2])], axis=0
+    ).reshape(12, plane)
 
     shape = (3, length_x, length_z, length_y)
     x_face, z_face = (3, length_z, length_y), (3, length_x, length_y)
-    outs = [shape, shape, x_face, x_face, z_face, z_face, (8, length_y)]
-
-    def apply(comp, field, left_ref, right_ref, cols, share, sums):
-        both = dot(field, right_ref[...])
-        stacked = jnp.concatenate([both[:, :length_y], both[:, length_y:]], axis=0)
+    halo = [shape, x_face, x_face, z_face, z_face]
+
+    def apply(fields, left_ref, right_ref):
+        both = dot(jnp.concatenate(fields, axis=0), right_ref[...])
+        parts = [both[c * plane : (c + 1) * plane] for c in range(3)]
+        stacked = jnp.concatenate(
+            [
+                jnp.concatenate([part[:, :length_y] for part in parts], axis=1),
+                jnp.concatenate([part[:, length_y:] for part in parts], axis=1),
+            ],
+            axis=0,
+        )
         applied = dot(left_ref[...], stacked)
-        sums[comp : comp + 1, :] = share[...] * jnp.sum(
-            field * field * cols[:, 0:1], axis=0, keepdims=True
-        )
-        sums[comp + 3 : comp + 4, :] = share[...] * jnp.sum(
-            field * applied * cols[:, 1:2], axis=0, keepdims=True
-        )
-        return applied
-
-    def store(comp, field, applied, u, t, xl, xh, zl, zh):
-        u[comp] = field.reshape(length_x, length_z, length_y)
+        return [applied[:, c * length_y : (c + 1) * length_y] for c in range(3)]
+
+    def total(first, second, weight, share):
+        return share[...] * jnp.sum(first * second * weight, axis=0, keepdims=True)
+
+    def store(comp, applied, t, xl, xh, zl, zh):
         cube = applied.reshape(length_x, length_z, length_y)
         t[comp] = cube
         xl[comp] = cube[0]
@@ -286,36 +294,14 @@
         zl[comp] = cube[:, 0, :]
         zh[comp] = cube[:, length_z - 1, :]
 
-    spread_pick = np.zeros((2 * length_z + 2 * length_x, plane))
-    for z in range(length_z):
-        spread_pick[z, z] = 1.0
-        spread_pick[length_z + z, plane - length_z + z] = 1.0
-    for x in range(length_x):
-        spread_pick[2 * length_z + x, x * length_z] = 1.0
-        spread_pick[2 * length_z + length_x + x, x * length_z + length_z - 1] = 1.0
-    spread_pick = jnp.asarray(spread_pick, jnp.float32)
-
-    def first_kernel(
-        v, trac, xp, xn, zp, zn, place, left_ref, right_ref, cols, share,
-        u, t, xl, xh, zl, zh, sums,
-    ):
-        edge = jnp.concatenate([xp[...], xn[...], zp[...], zn[...]], axis=1)
-        wall = trac[...] + dot(edge, place[...])
-        wall = jnp.concatenate([wall, jnp.zeros((4, plane), jnp.float32)], axis=0)
-        wall = jnp.transpose(wall)
-        lane = lax.broadcasted_iota(jnp.int32, (plane, length_y), 1)
+    def smooth_part(comp, v, cols, right_ref):
         tall_y = jnp.sum(right_ref[:, length_y:], axis=0, keepdims=True)
-        sums[...] = jnp.zeros((8, length_y), jnp.float32)
-        for comp in range(3):
-            field = v[comp].reshape(plane, length_y) * (cols[:, 2:3] * tall_y)
-            if comp != 1:
-                at = comp
-                field = field + jnp.where(lane == 0, wall[:, at : at + 1], 0.0)
-                field = field + jnp.where(
-                    lane == length_y - 1, wall[:, at + 1 : at + 2], 0.0
-                )
-            applied = apply(comp, field, left_ref, right_ref, cols, share, sums)
-            store(comp, field, applied, u, t, xl, xh, zl, zh)
+        return v[comp].reshape(plane, length_y) * (cols[:, 2:3] * tall_y)
+
+    def first_kernel(v, left_ref, right_ref, cols, t, xl, xh, zl, zh):
+        fields = [smooth_part(comp, v, cols, right_ref) for comp in range(3)]
+        for comp, applied in enumerate(apply(fields, left_ref, right_ref)):
+            store(comp, applied, t, xl, xh, zl, zh)
 
     def add_faces(comp, t_in, xp, xn, zp, zn):
         cube = t_in[comp]
@@ -328,30 +314,54 @@
         return cube.reshape(plane, length_y)
 
     def next_kernel(
-        t_in, xp, xn, zp, zn, left_ref, right_ref, cols, share, u, t, xl, xh, zl, zh, sums
+        v, wall_in, t_in, xp, xn, zp, zn, left_ref, right_ref, cols, share,
+        u0, u1, t, xl, xh, zl, zh, sums,
     ):
-        sums[...] = jnp.zeros((8, length_y), jnp.float32)
+        wall = jnp.concatenate([wall_in[...], jnp.zeros((4, plane), jnp.float32)], axis=0)
+        wall = jnp.transpose(wall)
+        lane = lax.broadcasted_iota(jnp.int32, (plane, length_y), 1)
+        sums[...] = jnp.zeros((16, length_y), jnp.float32)
+        fields = []
         for comp in range(3):
+            base = smooth_part(comp, v, cols, right_ref)
             field = add_faces(comp, t_in, xp, xn, zp, zn)
-            applied = apply(comp, field, left_ref, right_ref, cols, share, sums)
-            store(comp, field, applied, u, t, xl, xh, zl, zh)
+            if comp != 1:
+                for side, node in ((0, 0), (1, length_y - 1)):
+                    at = comp + side
+                    base = base + jnp.where(lane == node, wall[:, at : at + 1], 0.0)
+                    line = right_ref[node : node + 1, :]
+                    field = field + wall[:, at + 4 : at + 5] * line[:, :length_y]
+                    field = field + wall[:, at + 8 : at + 9] * line[:, length_y:]
+            u0[comp] = base.reshape(length_x, length_z, length_y)
+            u1[comp] = field.reshape(length_x, length_z, length_y)
+            weight = cols[:, 0:1]
+            sums[comp : comp + 1, :] = total(base, base, weight, share)
+            sums[comp + 3 : comp + 4, :] = total(base, field, weight, share)
+            sums[comp + 6 : comp + 7, :] = total(field, field, weight, share)
+            fields.append(field)
+        for comp, applied in enumerate(apply(fields, left_ref, right_ref)):
+            sums[comp + 9 : comp + 10, :] = total(fields[comp], applied, cols[:, 1:2], share)
+            store(comp, applied, t, xl, xh, zl, zh)
 
     devices = wall_count * lax.axis_size("span")
 
     def last_kernel(
-        t_in, xp, xn, zp, zn, left_ref, right_ref, cols, share, sums_0, sums_1, u, moments, sums
+        t_in, xp, xn, zp, zn, left_ref, right_ref, cols, share, sums_1, u, moments
     ):
-        sums[...] = jnp.zeros((8, length_y), jnp.float32)
-        for comp in range(3):
-            field = add_faces(comp, t_in, xp, xn, zp, zn)
-            apply(comp, field, left_ref, right_ref, cols, share, sums)
+        fields = [add_faces(comp, t_in, xp, xn, zp, zn) for comp in range(3)]
+        rows = [sums_1[...]]
+        for comp, field in enumerate(fields):
             u[comp] = field.reshape(length_x, length_z, length_y)
-        stacked = jnp.concatenate([sums_0[...], sums_1[...], sums[...]], axis=0)
-        total = jnp.sum(stacked, axis=1, keepdims=True)
+            rows.append(total(field, field, cols[:, 0:1], share))
+        for field, applied in zip(fields, apply(fields, left_ref, right_ref)):
+            rows.append(total(field, applied, cols[:, 1:2], share))
+        rows.append(jnp.zeros((2, length_y), jnp.float32))
+        stacked = jnp.concatenate(rows, axis=0)
+        summed = jnp.sum(stacked, axis=1, keepdims=True)
         row = lax.broadcasted_iota(jnp.int32, (24, 18), 0)
         col = lax.broadcasted_iota(jnp.int32, (24, 18), 1)
-        chosen = (row % 8 < 6) & (row // 8 * 6 + row % 8 == col)
-        line = jnp.sum(jnp.where(chosen, total, 0.0), axis=0, keepdims=True)
+        chosen = ((row < 12) & (row == col)) | ((row >= 16) & (row - 4 == col))
+        line = jnp.sum(jnp.where(chosen, summed, 0.0), axis=0, keepdims=True)
         moments[...] = jnp.broadcast_to(line, (devices, 18))
 
     def combine_kernel(moments, u0, u1, u2, out):
@@ -395,13 +405,13 @@
             ).reshape(length_x, length_z, length_y)
 
     tables = (left, right, columns, share_y)
-    u0, t0, *faces, sums_0 = call(
-        first_kernel, outs, velocity_old, traction, *around, spread_pick, *tables
-    )
-    u1, t1, *faces, sums_1 = call(next_kernel, outs, t0, *exchange(*faces), *tables)
-    u2, moments, _ = call(
-        last_kernel, [shape, (devices, 18), (8, length_y)],
-        t1, *exchange(*faces), *tables, sums_0, sums_1,
+    t0, *faces = call(first_kernel, halo, velocity_old, *tables[:3])
+    u0, u1, t1, *faces, sums_1 = call(
+        next_kernel, [shape, shape, *halo, (16, length_y)],
+        velocity_old, walls, t0, *exchange(*faces), *tables,
+    )
+    u2, moments = call(
+        last_kernel, [shape, (devices, 18)], t1, *exchange(*faces), *tables, sums_1
     )
     moments = lax.all_to_all(moments, ("wall", "span"), 0, 0, tiled=True)
     (answer,) = call(combine_kernel, [shape], moments, u0, u1, u2)

time: 81.2 us -> 74.7 us (0.920)
  waiting for transfers between devices: 17.2 us -> 11.5 us
  starting transfers between devices: 18.8 us -> 20.6 us
  local copies, waits for them, and re-layouts: 8.36 us -> 6.93 us
  Pallas kernels: 21.7 us -> 20.5 us
    ppermute x14, waiting for transfers between devices: 17.2 us -> 11.5 us  [shifted(): return lax.ppermute(value, axis, pairs)]
    ppermute x14, starting transfers between devices: 18.8 us -> 20.6 us  [shifted(): return lax.ppermute(value, axis, pairs)]
    pallas_call x5, Pallas kernels: 21.7 us -> 20.5 us  [call(): pl.pallas_call(kernel, out_shape=[jax.ShapeDtypeStruct(shape, jnp.float32...]
    unnamed x54 -> x48, local copies, waits for them, and re-layouts: 5.38 us -> 4.48 us
    slice x6 -> x4, local copies, waits for them, and re-layouts: 1.65 us -> 0.76 us  [with_corners(): return jnp.concatenate([first, face[:, 1:-1], last], axis=1)]
  transfers between devices with their start and end apart: 14 -> 14, of which waited for: 10 -> 6; matrix products, arithmetic and copies ran while one was open for 4% -> 5% of each run, Pallas kernels for 0% -> 7%
where the time goes in v2:
time: 74.7 us; the launch traced here: 74.1 us
  starting transfers between devices  20.6 us (28%)
  Pallas kernels  20.5 us (27%)
  waiting for transfers between devices  11.5 us (15%)
  blocking collectives  10.1 us (14%)
  local copies, waits for them, and re-layouts  6.93 us (9%)
  other arithmetic  2.79 us (4%)
  between operations  0.93 us (1%)
    ppermute x14, starting transfers between devices, shifted(): return lax.ppermute(value, axis, pairs)  20.6 us
    pallas_call x5, Pallas kernels, call(): pl.pallas_call(kernel, out_shape=[jax.ShapeDtypeStruct(shape, jnp.float32...  20.5 us
    ppermute x14, waiting for transfers between devices, shifted(): return lax.ppermute(value, axis, pairs)  11.5 us
    all_to_all x1, blocking collectives, body(): moments = lax.all_to_all(moments, ('wall', 'span'), 0, 0, tiled=True)  10.1 us
    unnamed x48, local copies, waits for them, and re-layouts  4.48 us
  transfers between devices with their start and end apart: 14, of which 6 were waited for; matrix products, arithmetic and copies ran while one was open for 5% of the time, Pallas kernels for 7%

profile of v2, /device:TPU:0, one launch (start us, length us, event | category | flops | bytes accessed | tf_op | source)
XLA Modules:
  0.0 74.1 jit_solution(16984959983854154219)
XLA Ops:
  0.6 1.0 %slice_bitcast_fusion = (f32[8,16,128]{2,1,0:T(8,128)S(1)}, f32[8,16,128]{2,1,0:T(8,128)S(1)}, f32[8,16,128]{2,1,0:T(8,128)S(1)}, f32[8,16,128]{2,1,0:T(8,128)S(1)}) fusion(f32[3,16,16,128]{3,2,1,0:T(8,128)} %v.3), kind=kLoop, calls=%fused_computation.7 | loop fusion | bytes 524288 | tf_op jit(solution)/shard_map/squeeze | solution.py:170
  2.0 3.4 %collective-permute-start.1 = (f32[128,128]{1,0:T(8,128)S(1)}, f32[128,128]{1,0:T(8,128)S(1)}, u32[]{:S(2)}, u32[]{:S(2)}) collective-permute-start(f32[128,128]{1,0:T(8,128)S(1)} %bitcast.51), channel_id=1, source_target_pairs={{0,28},{4,0},{8,4},{12,8},{16,12},{20,16},{24,20},{28,24},{1,29},{... | collective-permute-start | bytes 196616 | tf_op jit(solution)/shard_map/ppermute | solution.py:45
  5.5 0.7 fusion.right_ref
  6.2 4.9 %shard_map.150 = (f32[3,16,16,128]{3,2,1,0:T(8,128)}, f32[3,16,128]{2,1,0:T(8,128)}, f32[3,16,128]{2,1,0:T(8,128)}, f32[3,16,128]{2,1,0:T(8,128)}, f32[3,16,128]{2,1,0:T(8,128)}) custom-call(f32[3,16,16,128]{3,2,1,0:T(8,128)} %v.3, f32[256,512]{1,0:T(8,128)} %constant.65.clone.left_ref, f32[128,256]{1,0:T(8,128)} %fusion.right_ref, f32[256,8]{1,0:T(8,128)} %constant.68.clone.cols), custom_call_target="tpu_custom_call" | custom-call | tf_op jit(solution)/shard_map/pallas_call | solution.py:104
  11.1 2.7 %collective-permute-start.7 = (f32[3,16,128]{2,1,0:T(8,128)}, f32[3,16,128]{2,1,0:T(8,128)S(1)}, u32[]{:S(2)}, u32[]{:S(2)}) collective-permute-start(f32[3,16,128]{2,1,0:T(8,128)} %get-tuple-element.22), channel_id=1, source_target_pairs={{0,28},{4,0},{8,4},{12,8},{16,12},{20,16},{24,20},{28,24},{1,29},{... | collective-permute-start | bytes 73736 | tf_op jit(solution)/shard_map/ppermute | solution.py:45
  13.9 0.6 copy-done.18
  14.5 0.6 pad_maximum_fusion.4.info
  15.1 0.7 copy-done.5
  16.0 0.6 copy-done.3
  16.6 0.6 copy-done.4
  17.2 3.0 %shard_map.149 = (f32[2,512]{1,0:T(2,128)}, f32[4,256]{1,0:T(4,128)}) custom-call(f32[128,128]{1,0:T(8,128)} %bitcast.53, f32[128,128]{1,0:T(8,128)} %copy-done.4, f32[128,128]{1,0:T(8,128)} %copy-done.3, f32[6,512]{1,0:T(8,128)} %pad_maximum_fusion.4.info, f32[1,256]{1,0:T(1,128)} %constant.70.clone.mass), custom_call_target="tpu_custom_call" | custom-call | tf_op jit(solution)/shard_map/pallas_call | solution.py:104
  20.1 2.3 %collective-permute-start.3 = (f32[4,256]{1,0:T(4,128)}, f32[4,256]{1,0:T(4,128)S(1)}, u32[]{:S(2)}, u32[]{:S(2)}) collective-permute-start(f32[4,256]{1,0:T(4,128)} %get-tuple-element.19), channel_id=1, source_target_pairs={{0,28},{4,0},{8,4},{12,8},{16,12},{20,16},{24,20},{28,24},{1,29},{... | collective-permute-start | bytes 12296 | tf_op jit(solution)/shard_map/ppermute | solution.py:45
  22.5 3.7 %collective-permute-start.9 = (f32[3,16,128]{2,1,0:T(8,128)S(1)}, f32[3,16,128]{2,1,0:T(8,128)S(1)}, u32[]{:S(2)}, u32[]{:S(2)}) collective-permute-start(f32[3,16,128]{2,1,0:T(8,128)S(1)} %pad_maximum_fusion.1), channel_id=1, source_target_pairs={{0,3},{1,0},{2,1},{3,2},{4,7},{5,4},{6,5},{7,6},{8,11},{9,8},{10,9... | collective-permute-start | bytes 73736 | tf_op jit(solution)/shard_map/ppermute | solution.py:45
  26.7 0.6 copy-done.13
  27.6 3.7 %collective-permute-start.5 = (f32[3,4,16,16]{3,2,0,1:T(8,128)S(1)}, f32[3,4,16,16]{3,2,0,1:T(8,128)S(1)}, u32[]{:S(2)}, u32[]{:S(2)}) collective-permute-start(f32[3,4,16,16]{3,2,0,1:T(8,128)S(1)} %convolution_bitcast_fusion.1), channel_id=1, source_target_pairs={{0,3},{1,0},{2,1},{3,2},{4,7},{5,4},{6,5},{7,6},{8,11},{9,8},{10,9... | collective-permute-start | bytes 36872 | tf_op jit(solution)/shard_map/ppermute | solution.py:45
  31.3 2.1 %collective-permute-done.5 = f32[3,4,16,16]{3,2,0,1:T(8,128)S(1)} collective-permute-done((f32[3,4,16,16]{3,2,0,1:T(8,128)S(1)}, f32[3,4,16,16]{3,2,0,1:T(8,128)S(1)}, u32[]{:S(2)}, u32[]{:S(2)}) %collective-permute-start.5) | collective-permute-done | bytes 12320 | tf_op jit(solution)/shard_map/ppermute | solution.py:45
  33.5 4.2 %collective-permute-done.4 = f32[3,4,16,16]{3,2,0,1:T(8,128)S(1)} collective-permute-done((f32[3,4,16,16]{3,2,0,1:T(8,128)S(1)}, f32[3,4,16,16]{3,2,0,1:T(8,128)S(1)}, u32[]{:S(2)}, u32[]{:S(2)}) %collective-permute-start.4) | collective-permute-done | bytes 12320 | tf_op jit(solution)/shard_map/ppermute | solution.py:45
  37.7 0.5 convolution_bitcast_fusion
  38.4 0.6 pad_maximum_fusion.5.wall_in
  39.1 0.6 copy-done.14
  39.7 5.5 %shard_map.151 = (f32[3,16,16,128]{3,2,1,0:T(8,128)}, f32[3,16,16,128]{3,2,1,0:T(8,128)}, f32[3,16,16,128]{3,2,1,0:T(8,128)}, f32[3,16,128]{2,1,0:T(8,128)}, f32...) custom-call(f32[3,16,16,128]{3,2,1,0:T(8,128)} %v.3, ...), custom_call_target="tpu_custom_call" | custom-call | tf_op jit(solution)/shard_map/pallas_call | solution.py:104
  45.2 2.6 %collective-permute-start.11 = (f32[3,16,128]{2,1,0:T(8,128)}, f32[3,16,128]{2,1,0:T(8,128)S(1)}, u32[]{:S(2)}, u32[]{:S(2)}) collective-permute-start(f32[3,16,128]{2,1,0:T(8,128)} %get-tuple-element.27), channel_id=1, source_target_pairs={{0,28},{4,0},{8,4},{12,8},{16,12},{20,16},{24,20},{28,24},{1,29},{... | collective-permute-start | bytes 73736 | tf_op jit(solution)/shard_map/ppermute | solution.py:45
  47.8 0.7 %slice.136 = f32[3,14,128]{2,1,0:T(8,128)S(1)} slice(f32[3,16,128]{2,1,0:T(8,128)} %get-tuple-element.28), slice={[0:3], [1:15], [0:128]} | slice | bytes 43008 | tf_op jit(solution)/shard_map/slice | solution.py:95
  48.6 1.0 %collective-permute-done.10.xp = f32[3,16,128]{2,1,0:T(8,128)S(1)} collective-permute-done((f32[3,16,128]{2,1,0:T(8,128)}, f32[3,16,128]{2,1,0:T(8,128)S(1)}, u32[]{:S(2)}, u32[]{:S(2)}) %collective-permute-start.10) | collective-permute-done | bytes 24608 | tf_op jit(solution)/shard_map/ppermute | solution.py:45
  49.6 0.7 slice_add_fusion.2
  50.5 2.0 %collective-permute-start.12 = (f32[3,16,128]{2,1,0:T(8,128)S(1)}, f32[3,16,128]{2,1,0:T(8,128)S(1)}, u32[]{:S(2)}, u32[]{:S(2)}) collective-permute-start(f32[3,16,128]{2,1,0:T(8,128)S(1)} %pad_maximum_fusion.2), channel_id=1, source_target_pairs={{0,1},{1,2},{2,3},{3,0},{4,5},{5,6},{6,7},{7,4},{8,9},{9,10},{10,1... | collective-permute-start | bytes 73736 | tf_op jit(solution)/shard_map/ppermute | solution.py:45
  52.5 1.7 %collective-permute-done.13.zn = f32[3,16,128]{2,1,0:T(8,128)S(1)} collective-permute-done((f32[3,16,128]{2,1,0:T(8,128)S(1)}, f32[3,16,128]{2,1,0:T(8,128)S(1)}, u32[]{:S(2)}, u32[]{:S(2)}) %collective-permute-start.13) | collective-permute-done | bytes 24608 | tf_op jit(solution)/shard_map/ppermute | solution.py:45
  54.2 2.0 %collective-permute-done.12.zp = f32[3,16,128]{2,1,0:T(8,128)S(1)} collective-permute-done((f32[3,16,128]{2,1,0:T(8,128)S(1)}, f32[3,16,128]{2,1,0:T(8,128)S(1)}, u32[]{:S(2)}, u32[]{:S(2)}) %collective-permute-start.12) | collective-permute-done | bytes 24608 | tf_op jit(solution)/shard_map/ppermute | solution.py:45
  56.2 0.6 copy-done.17
  56.8 4.8 %shard_map.152 = (f32[3,16,16,128]{3,2,1,0:T(8,128)}, f32[32,18]{1,0:T(8,128)}) custom-call(f32[3,16,16,128]{3,2,1,0:T(8,128)} %get-tuple-element.25.t_in, f32[3,16,128]{2,1,0:T(8,128)} %copy-done.10, f32[3,16,128]{2,1,0:T(8,128)} %copy-done.11, f32[3,16,128]{2,1,0:T(8,128)} %copy-done.17, f32[3,16,128]{2,1,0:T(8,128)} %copy-done.16, ...), custom_call_target="tpu_custom_call" | custom-call | tf_op jit(solution)/shard_map/pallas_call | solution.py:104
  61.6 10.1 %all_to_all.11 = f32[32,1,18]{2,1,0:T(1,128)} all-to-all(f32[32,1,18]{2,1,0:T(1,128)} %bitcast.55), channel_id=1, replica_groups=mesh['wall'=8,'span'=4] {'wall','span'}, dimensions={0} | all-to-all | bytes 4608 | tf_op jit(solution)/shard_map/all_to_all | solution.py:416
  71.8 2.3 %shard_map.153 = f32[3,16,16,128]{3,2,1,0:T(8,128)} custom-call(f32[32,18]{1,0:T(8,128)} %bitcast.54, f32[3,16,16,128]{3,2,1,0:T(8,128)} %get-tuple-element.32.u0, f32[3,16,16,128]{3,2,1,0:T(8,128)} %get-tuple-element.33.u1, f32[3,16,16,128]{3,2,1,0:T(8,128)} %get-tuple-element.34.u2), custom_call_target="tpu_custom_call" | custom-call | tf_op jit(solution)/shard_map/pallas_call | solution.py:104
  (77 shorter events, 1.9 us)
Async XLA Ops:
  1.8 3.7 %copy-start.1 = (f32[16,8,256]{2,1,0:T(8,128)S(1)}, f32[16,8,256]{2,1,0:T(8,128)}, u32[]{:S(2)}) copy-start(f32[16,8,256]{2,1,0:T(8,128)} %constant.67.clone) | copy-start | bytes 393220
  1.8 3.7 %copy-start.2 = (f32[16,8,256]{2,1,0:T(8,128)S(1)}, f32[16,8,256]{2,1,0:T(8,128)}, u32[]{:S(2)}) copy-start(f32[16,8,256]{2,1,0:T(8,128)} %constant.66.clone) | copy-start | bytes 393220
  2.0 4.2 %copy-start = (f32[8,16,128]{2,1,0:T(8,128)}, f32[8,16,128]{2,1,0:T(8,128)S(1)}, u32[]{:S(2)}) copy-start(f32[8,16,128]{2,1,0:T(8,128)S(1)} %concatenate.32) | copy-start | bytes 196612
  2.0 3.4 %copy-start.23 = (f32[16]{0:T(128)S(1)}, f32[16]{0:T(128)}, u32[]{:S(2)}) copy-start(f32[16]{0:T(128)} %param.15) | copy-start | bytes 196
  2.0 13.9 %collective-permute-start.1 = (f32[128,128]{1,0:T(8,128)S(1)}, f32[128,128]{1,0:T(8,128)S(1)}, u32[]{:S(2)}, u32[]{:S(2)}) collective-permute-start(f32[128,128]{1,0:T(8,128)S(1)} %bitcast.51), channel_id=1, source_target_pairs={{0,28},{4,0},{8,4},{12,8},{16,12},{20,16},{24,20},{28,24},{1,29},{... | collective-permute-start | bytes 196616 | tf_op jit(solution)/shard_map/ppermute | solution.py:45
  5.5 10.5 %collective-permute-start = (f32[128,128]{1,0:T(8,128)S(1)}, f32[128,128]{1,0:T(8,128)S(1)}, u32[]{:S(2)}, u32[]{:S(2)}) collective-permute-start(f32[128,128]{1,0:T(8,128)S(1)} %bitcast.52), channel_id=1, source_target_pairs={{0,4},{4,8},{8,12},{12,16},{16,20},{20,24},{24,28},{28,0},{1,5},{5... | collective-permute-start | bytes 196616 | tf_op jit(solution)/shard_map/ppermute | solution.py:45
  6.2 7.6 %copy-start.20 = (s32[512,1]{0,1:T(1,128)S(1)}, s32[512,1]{0,1:T(1,128)}, u32[]{:S(2)}) copy-start(s32[512,1]{0,1:T(1,128)} %param.17) | copy-start | bytes 6148
  6.2 7.6 %copy-start.21 = (s32[512,1]{0,1:T(1,128)S(1)}, s32[512,1]{0,1:T(1,128)}, u32[]{:S(2)}) copy-start(s32[512,1]{0,1:T(1,128)} %param.16) | copy-start | bytes 6148
  6.2 7.7 %copy-start.22 = (f32[512]{0:T(512)S(1)}, f32[512]{0:T(512)}, u32[]{:S(2)}) copy-start(f32[512]{0:T(512)} %param.19) | copy-start | bytes 6148
  11.1 4.7 %collective-permute-start.6 = (f32[3,16,128]{2,1,0:T(8,128)}, f32[3,16,128]{2,1,0:T(8,128)S(1)}, u32[]{:S(2)}, u32[]{:S(2)}) collective-permute-start(f32[3,16,128]{2,1,0:T(8,128)} %get-tuple-element.21), channel_id=1, source_target_pairs={{0,4},{4,8},{8,12},{12,16},{16,20},{20,24},{24,28},{28,0},{1,5},{5... | collective-permute-start | bytes 73736 | tf_op jit(solution)/shard_map/ppermute | solution.py:45
  11.1 4.8 %collective-permute-start.7 = (f32[3,16,128]{2,1,0:T(8,128)}, f32[3,16,128]{2,1,0:T(8,128)S(1)}, u32[]{:S(2)}, u32[]{:S(2)}) collective-permute-start(f32[3,16,128]{2,1,0:T(8,128)} %get-tuple-element.22), channel_id=1, source_target_pairs={{0,28},{4,0},{8,4},{12,8},{16,12},{20,16},{24,20},{28,24},{1,29},{... | collective-permute-start | bytes 73736 | tf_op jit(solution)/shard_map/ppermute | solution.py:45
  13.8 1.3 %copy-start.6 = (f32[3,16,128]{2,1,0:T(8,128)S(1)}, f32[3,16,128]{2,1,0:T(8,128)}, u32[]{:S(2)}) copy-start(f32[3,16,128]{2,1,0:T(8,128)} %get-tuple-element.23) | copy-start | bytes 73732
  15.1 0.7 copy-start.5
  15.9 4.3 %copy-start.8 = (f32[3,16,128]{2,1,0:T(8,128)}, f32[3,16,128]{2,1,0:T(8,128)S(1)}, u32[]{:S(2)}) copy-start(f32[3,16,128]{2,1,0:T(8,128)S(1)} %collective-permute-done.6.xp) | copy-start | bytes 73732
  15.9 4.3 %copy-start.9 = (f32[3,16,128]{2,1,0:T(8,128)}, f32[3,16,128]{2,1,0:T(8,128)S(1)}, u32[]{:S(2)}) copy-start(f32[3,16,128]{2,1,0:T(8,128)S(1)} %collective-permute-done.7.xn) | copy-start | bytes 73732
  20.1 6.0 %collective-permute-start.3 = (f32[4,256]{1,0:T(4,128)}, f32[4,256]{1,0:T(4,128)S(1)}, u32[]{:S(2)}, u32[]{:S(2)}) collective-permute-start(f32[4,256]{1,0:T(4,128)} %get-tuple-element.19), channel_id=1, source_target_pairs={{0,28},{4,0},{8,4},{12,8},{16,12},{20,16},{24,20},{28,24},{1,29},{... | collective-permute-start | bytes 12296 | tf_op jit(solution)/shard_map/ppermute | solution.py:45
  22.5 4.1 %collective-permute-start.2 = (f32[4,256]{1,0:T(4,128)}, f32[4,256]{1,0:T(4,128)S(1)}, u32[]{:S(2)}, u32[]{:S(2)}) collective-permute-start(f32[4,256]{1,0:T(4,128)} %get-tuple-element.19), channel_id=1, source_target_pairs={{0,4},{4,8},{8,12},{12,16},{16,20},{20,24},{24,28},{28,0},{1,5},{5... | collective-permute-start | bytes 12296 | tf_op jit(solution)/shard_map/ppermute | solution.py:45
  22.5 4.1 %copy-start.19 = (f32[4,256]{1,0:T(4,128)S(1)}, f32[4,256]{1,0:T(4,128)}, u32[]{:S(2)}) copy-start(f32[4,256]{1,0:T(4,128)} %get-tuple-element.19) | copy-start | bytes 12292
  22.5 16.6 %collective-permute-start.9 = (f32[3,16,128]{2,1,0:T(8,128)S(1)}, f32[3,16,128]{2,1,0:T(8,128)S(1)}, u32[]{:S(2)}, u32[]{:S(2)}) collective-permute-start(f32[3,16,128]{2,1,0:T(8,128)S(1)} %pad_maximum_fusion.1), channel_id=1, source_target_pairs={{0,3},{1,0},{2,1},{3,2},{4,7},{5,4},{6,5},{7,6},{8,11},{9,8},{10,9... | collective-permute-start | bytes 73736 | tf_op jit(solution)/shard_map/ppermute | solution.py:45
  26.6 0.7 %copy-start.13 = (f32[3,16,48,1]{2,1,0,3:T(8,128)S(1)}, f32[3,16,48,1]{2,1,0,3:T(8,128)}, u32[]{:S(2)}) copy-start(f32[3,16,48,1]{2,1,0,3:T(8,128)} %constant.73) | copy-start | bytes 27652
  27.6 5.9 %collective-permute-start.5 = (f32[3,4,16,16]{3,2,0,1:T(8,128)S(1)}, f32[3,4,16,16]{3,2,0,1:T(8,128)S(1)}, u32[]{:S(2)}, u32[]{:S(2)}) collective-permute-start(f32[3,4,16,16]{3,2,0,1:T(8,128)S(1)} %convolution_bitcast_fusion.1), channel_id=1, source_target_pairs={{0,3},{1,0},{2,1},{3,2},{4,7},{5,4},{6,5},{7,6},{8,11},{9,8},{10,9... | collective-permute-start | bytes 36872 | tf_op jit(solution)/shard_map/ppermute | solution.py:45
  31.3 6.4 %collective-permute-start.4 = (f32[3,4,16,16]{3,2,0,1:T(8,128)S(1)}, f32[3,4,16,16]{3,2,0,1:T(8,128)S(1)}, u32[]{:S(2)}, u32[]{:S(2)}) collective-permute-start(f32[3,4,16,16]{3,2,0,1:T(8,128)S(1)} %convolution_bitcast_fusion.1), channel_id=1, source_target_pairs={{0,1},{1,2},{2,3},{3,0},{4,5},{5,6},{6,7},{7,4},{8,9},{9,10},{10,1... | collective-permute-start | bytes 36872 | tf_op jit(solution)/shard_map/ppermute | solution.py:45
  31.3 6.4 %copy-start.12 = (f32[3,16,48,1,1]{2,1,0,4,3:T(8,128)S(1)}, f32[3,16,48,1,1]{2,1,0,4,3:T(8,128)}, u32[]{:S(2)}) copy-start(f32[3,16,48,1,1]{2,1,0,4,3:T(8,128)} %constant.74) | copy-start | bytes 27652
  31.3 7.8 %collective-permute-start.8 = (f32[3,16,128]{2,1,0:T(8,128)S(1)}, f32[3,16,128]{2,1,0:T(8,128)S(1)}, u32[]{:S(2)}, u32[]{:S(2)}) collective-permute-start(f32[3,16,128]{2,1,0:T(8,128)S(1)} %pad_maximum_fusion), channel_id=1, source_target_pairs={{0,1},{1,2},{2,3},{3,0},{4,5},{5,6},{6,7},{7,4},{8,9},{9,10},{10,1... | collective-permute-start | bytes 73736 | tf_op jit(solution)/shard_map/ppermute | solution.py:45
  45.1 4.4 %collective-permute-start.10 = (f32[3,16,128]{2,1,0:T(8,128)}, f32[3,16,128]{2,1,0:T(8,128)S(1)}, u32[]{:S(2)}, u32[]{:S(2)}) collective-permute-start(f32[3,16,128]{2,1,0:T(8,128)} %get-tuple-element.26), channel_id=1, source_target_pairs={{0,4},{4,8},{8,12},{12,16},{16,20},{20,24},{24,28},{28,0},{1,5},{5... | collective-permute-start | bytes 73736 | tf_op jit(solution)/shard_map/ppermute | solution.py:45
  45.2 4.4 %collective-permute-start.11 = (f32[3,16,128]{2,1,0:T(8,128)}, f32[3,16,128]{2,1,0:T(8,128)S(1)}, u32[]{:S(2)}, u32[]{:S(2)}) collective-permute-start(f32[3,16,128]{2,1,0:T(8,128)} %get-tuple-element.27), channel_id=1, source_target_pairs={{0,28},{4,0},{8,4},{12,8},{16,12},{20,16},{24,20},{28,24},{1,29},{... | collective-permute-start | bytes 73736 | tf_op jit(solution)/shard_map/ppermute | solution.py:45
  47.8 0.8 %copy-start.7 = (f32[3,16,128]{2,1,0:T(8,128)S(1)}, f32[3,16,128]{2,1,0:T(8,128)}, u32[]{:S(2)}) copy-start(f32[3,16,128]{2,1,0:T(8,128)} %get-tuple-element.29) | copy-start | bytes 73732
  49.5 0.8 %copy-start.10 = (f32[3,16,128]{2,1,0:T(8,128)}, f32[3,16,128]{2,1,0:T(8,128)S(1)}, u32[]{:S(2)}) copy-start(f32[3,16,128]{2,1,0:T(8,128)S(1)} %collective-permute-done.10.xp) | copy-start | bytes 73732
  49.6 0.8 %copy-start.11 = (f32[3,16,128]{2,1,0:T(8,128)}, f32[3,16,128]{2,1,0:T(8,128)S(1)}, u32[]{:S(2)}) copy-start(f32[3,16,128]{2,1,0:T(8,128)S(1)} %collective-permute-done.11.xn) | copy-start | bytes 73732
  50.3 3.9 %collective-permute-start.13 = (f32[3,16,128]{2,1,0:T(8,128)S(1)}, f32[3,16,128]{2,1,0:T(8,128)S(1)}, u32[]{:S(2)}, u32[]{:S(2)}) collective-permute-start(f32[3,16,128]{2,1,0:T(8,128)S(1)} %pad_maximum_fusion.3), channel_id=1, source_target_pairs={{0,3},{1,0},{2,1},{3,2},{4,7},{5,4},{6,5},{7,6},{8,11},{9,8},{10,9... | collective-permute-start | bytes 73736 | tf_op jit(solution)/shard_map/ppermute | solution.py:45
  50.5 5.7 %collective-permute-start.12 = (f32[3,16,128]{2,1,0:T(8,128)S(1)}, f32[3,16,128]{2,1,0:T(8,128)S(1)}, u32[]{:S(2)}, u32[]{:S(2)}) collective-permute-start(f32[3,16,128]{2,1,0:T(8,128)S(1)} %pad_maximum_fusion.2), channel_id=1, source_target_pairs={{0,1},{1,2},{2,3},{3,0},{4,5},{5,6},{6,7},{7,4},{8,9},{9,10},{10,1... | collective-permute-start | bytes 73736 | tf_op jit(solution)/shard_map/ppermute | solution.py:45
  54.2 2.0 %copy-start.16 = (f32[3,16,128]{2,1,0:T(8,128)}, f32[3,16,128]{2,1,0:T(8,128)S(1)}, u32[]{:S(2)}) copy-start(f32[3,16,128]{2,1,0:T(8,128)S(1)} %collective-permute-done.13.zn) | copy-start | bytes 73732
  (6 other events, 3.7 us)

commit v3 on v2

--- a/solution.py
+++ b/solution.py
@@ -85,17 +85,17 @@
     return table
 
 
+def face_corners(face, from_prev, from_next, spot):
+    first = face[:, :1] + from_prev[:, spot]
+    last = face[:, -1:] + from_next[:, spot]
+    return jnp.concatenate([first, face[:, 1:-1], last], axis=1)
+
+
 def exchange(x_low, x_high, z_low, z_high):
     from_prev = shifted(x_high, "wall", 1)
     from_next = shifted(x_low, "wall", -1)
-
-    def with_corners(face, spot):
-        first = face[:, :1] + from_prev[:, spot]
-        last = face[:, -1:] + from_next[:, spot]
-        return jnp.concatenate([first, face[:, 1:-1], last], axis=1)
-
-    z_low = with_corners(z_low, slice(0, 1))
-    z_high = with_corners(z_high, slice(-1, None))
+    z_low = face_corners(z_low, from_prev, from_next, slice(0, 1))
+    z_high = face_corners(z_high, from_prev, from_next, slice(-1, None))
     return from_prev, from_next, shifted(z_high, "span", 1), shifted(z_low, "span", -1)
 
 
@@ -127,14 +127,19 @@
     mass_z = np.tile(0.5 * element_dz * weights, count_z)
     stiff_x = np.kron(np.eye(count_x), stiffness * (2.0 / element_dx))
     stiff_z = np.kron(np.eye(count_z), stiffness * (2.0 / element_dz))
-    join_x, join_z, join_y = (join_matrix(n) for n in (length_x, length_z, length_y))
-    join_xz = np.kron(join_x, join_z)
+    join_z, join_y = (join_matrix(n) for n in (length_z, length_y))
+    slab = 8 * length_z
     mass_xz = np.kron(mass_x, mass_z)
-    plane_op = viscosity * (
-        np.kron(stiff_x, np.diag(mass_z)) + np.kron(np.diag(mass_x), stiff_z)
+    mass_a, stiff_a = mass_x[:8], stiff_x[:8, :8]
+    join_slab = np.kron(np.eye(8), join_z)
+    slab_op = viscosity * (
+        np.kron(stiff_a, np.diag(mass_z)) + np.kron(np.diag(mass_a), stiff_z)
     )
     left = jnp.asarray(
-        np.concatenate([join_xz @ np.diag(mass_xz), join_xz @ plane_op], axis=1), jnp.float32
+        np.concatenate(
+            [join_slab @ np.diag(np.kron(mass_a, mass_z)), join_slab @ slab_op], axis=1
+        ),
+        jnp.float32,
     )
     tiled = np.tile(weights, count_y)
     stiff_part = np.concatenate(
@@ -163,18 +168,6 @@
     columns = jnp.asarray(columns, jnp.float32)
     share_y = jnp.asarray(face_weights(length_y, True)[None, :], jnp.float32)
 
-    def packed_near():
-        pieces = []
-        for ex in range(count_x):
-            for comp in (0, 2):
-                block = velocity_old[comp, ex * 8 : ex * 8 + 8]
-                pieces.append(block[:, :, :near])
-                pieces.append(block[:, :, length_y - near :])
-        return jnp.concatenate(pieces, axis=2).reshape(8 * length_z, count_x * 4 * near)
-
-    own_near = packed_near()
-    prev_near = shifted(own_near, "wall", 1)
-    next_near = shifted(own_near, "wall", -1)
     wall_count = lax.axis_size("wall")
     own_wall = lax.axis_index("wall")
     distance = ((owner_device[:, 0] - own_wall + wall_count) % wall_count)[None, :]
@@ -223,8 +216,8 @@
             table = jnp.where(fits & (comp == k), full_y, 0.0)
             picked = jnp.where(
                 relation_row == 0.0,
-                dot(own[...], table),
-                jnp.where(relation_row > 0.0, dot(nxt[...], table), dot(prev[...], table)),
+                dot(own[:slab, :], table),
+                jnp.where(relation_row > 0.0, dot(nxt[:slab, :], table), dot(prev[:slab, :], table)),
             )
             sampled.append(jnp.sum(picked * mix, axis=0, keepdims=True))
         stream, spanwise = sampled
@@ -240,39 +233,15 @@
                 half.append(part * mass[...])
         trac[...] = jnp.concatenate(half, axis=0)
 
-    neumann, traction = call(
-        sample_kernel,
-        [(2, point_total), (4, plane)],
-        own_near, prev_near, next_near, per_point, mass_row,
-    )
-
-    def plane_tables(length, mass, stiff):
-        join = join_matrix(3 * length)
-        wide_mass = join @ np.diag(np.tile(mass, 3)) @ join
-        wide_stiff = join @ np.kron(np.eye(3), stiff) @ join
-        return np.stack([join, wide_mass, wide_stiff])[:, length : 2 * length]
-
-    ops_x = jnp.asarray(plane_tables(length_x, mass_x, stiff_x), jnp.float32)
-    ops_z = jnp.asarray(plane_tables(length_z, mass_z, stiff_z), jnp.float32)
-    wide = jnp.concatenate(
-        [shifted(traction, "wall", 1), traction, shifted(traction, "wall", -1)], axis=1
-    ).reshape(4, 3 * length_x, length_z)
-    along = jnp.einsum("oxs,csz->ocxz", ops_x, wide, precision=precise)
-    wide = jnp.concatenate(
-        [shifted(along, "span", 1), along, shifted(along, "span", -1)], axis=3
-    )
-    both = jnp.einsum("ocxs,pzs->opcxz", wide, ops_z, precision=precise)
-    walls = jnp.concatenate(
-        [both[0, 0], both[1, 1], viscosity * (both[2, 1] + both[1, 2])], axis=0
-    ).reshape(12, plane)
-
     shape = (3, length_x, length_z, length_y)
     x_face, z_face = (3, length_z, length_y), (3, length_x, length_y)
     halo = [shape, x_face, x_face, z_face, z_face]
+    face_rows = 3 * length_z
+    message = (slab + face_rows, length_y)
 
     def apply(fields, left_ref, right_ref):
         both = dot(jnp.concatenate(fields, axis=0), right_ref[...])
-        parts = [both[c * plane : (c + 1) * plane] for c in range(3)]
+        parts = [both[k * slab : (k + 1) * slab] for k in range(3 * count_x)]
         stacked = jnp.concatenate(
             [
                 jnp.concatenate([part[:, :length_y] for part in parts], axis=1),
@@ -281,7 +250,22 @@
             axis=0,
         )
         applied = dot(left_ref[...], stacked)
-        return [applied[:, c * length_y : (c + 1) * length_y] for c in range(3)]
+        joined = []
+        for c in range(3):
+            pieces = []
+            for ex in range(count_x):
+                k = c * count_x + ex
+                pieces.append(applied[:, k * length_y : (k + 1) * length_y])
+            rows = []
+            for ex, piece in enumerate(pieces):
+                first, last = piece[:length_z], piece[slab - length_z :]
+                if ex > 0:
+                    first = first + pieces[ex - 1][slab - length_z :]
+                if ex + 1 < count_x:
+                    last = last + pieces[ex + 1][:length_z]
+                rows += [first, piece[length_z : slab - length_z], last]
+            joined.append(jnp.concatenate(rows, axis=0))
+        return joined
 
     def total(first, second, weight, share):
         return share[...] * jnp.sum(first * second * weight, axis=0, keepdims=True)
@@ -298,10 +282,24 @@
         tall_y = jnp.sum(right_ref[:, length_y:], axis=0, keepdims=True)
         return v[comp].reshape(plane, length_y) * (cols[:, 2:3] * tall_y)
 
-    def first_kernel(v, left_ref, right_ref, cols, t, xl, xh, zl, zh):
+    def first_kernel(v, left_ref, right_ref, cols, t, low, high, zl, zh):
+        near_parts = []
+        for ex in range(count_x):
+            for comp in (0, 2):
+                block = v[comp, ex * 8 : ex * 8 + 8].reshape(slab, length_y)
+                near_parts += [block[:, :near], block[:, length_y - near :]]
+        near_all = jnp.concatenate(near_parts, axis=1)
+        low[:slab, :] = near_all
+        high[:slab, :] = near_all
         fields = [smooth_part(comp, v, cols, right_ref) for comp in range(3)]
         for comp, applied in enumerate(apply(fields, left_ref, right_ref)):
-            store(comp, applied, t, xl, xh, zl, zh)
+            cube = applied.reshape(length_x, length_z, length_y)
+            t[comp] = cube
+            at = slab + comp * length_z
+            low[at : at + length_z, :] = cube[0]
+            high[at : at + length_z, :] = cube[length_x - 1]
+            zl[comp] = cube[:, 0, :]
+            zh[comp] = cube[:, length_z - 1, :]
 
     def add_faces(comp, t_in, xp, xn, zp, zn):
         cube = t_in[comp]
@@ -405,10 +403,52 @@
             ).reshape(length_x, length_z, length_y)
 
     tables = (left, right, columns, share_y)
-    t0, *faces = call(first_kernel, halo, velocity_old, *tables[:3])
+    t0, low, high, z_low, z_high = call(
+        first_kernel, [shape, message, message, z_face, z_face], velocity_old, *tables[:3]
+    )
+    from_prev = shifted(high, "wall", 1)
+    from_next = shifted(low, "wall", -1)
+    neumann, traction = call(
+        sample_kernel,
+        [(2, point_total), (4, plane)],
+        low, from_prev, from_next, per_point, mass_row,
+    )
+
+    def plane_tables(length, mass, stiff):
+        join = join_matrix(3 * length)
+        wide_mass = join @ np.diag(np.tile(mass, 3)) @ join
+        wide_stiff = join @ np.kron(np.eye(3), stiff) @ join
+        return np.stack([join, wide_mass, wide_stiff])[:, length : 2 * length]
+
+    ops_x = jnp.asarray(plane_tables(length_x, mass_x, stiff_x), jnp.float32)
+    ops_z = jnp.asarray(plane_tables(length_z, mass_z, stiff_z), jnp.float32)
+    wide = jnp.concatenate(
+        [shifted(traction, "wall", 1), traction, shifted(traction, "wall", -1)], axis=1
+    ).reshape(4, 3 * length_x, length_z)
+    along = jnp.einsum("oxs,csz->ocxz", ops_x, wide, precision=precise)
+    size = along.size // length_y
+    along_rows = along.reshape(size, length_y)
+    x_prev = from_prev[slab:].reshape(x_face)
+    x_next = from_next[slab:].reshape(x_face)
+
+    def z_message(face, spot):
+        face = face_corners(face, x_prev, x_next, spot)
+        return jnp.concatenate([along_rows, face.reshape(3 * length_x, length_y)], axis=0)
+
+    z_prev = shifted(z_message(z_high, slice(-1, None)), "span", 1)
+    z_next = shifted(z_message(z_low, slice(0, 1)), "span", -1)
+    wide = jnp.concatenate(
+        [z_prev[:size].reshape(along.shape), along, z_next[:size].reshape(along.shape)], axis=3
+    )
+    around = (x_prev, x_next, z_prev[size:].reshape(z_face), z_next[size:].reshape(z_face))
+    both = jnp.einsum("ocxs,pzs->opcxz", wide, ops_z, precision=precise)
+    walls = jnp.concatenate(
+        [both[0, 0], both[1, 1], viscosity * (both[2, 1] + both[1, 2])], axis=0
+    ).reshape(12, plane)
+
     u0, u1, t1, *faces, sums_1 = call(
         next_kernel, [shape, shape, *halo, (16, length_y)],
-        velocity_old, walls, t0, *exchange(*faces), *tables,
+        velocity_old, walls, t0, *around, *tables,
     )
     u2, moments = call(
         last_kernel, [shape, (devices, 18)], t1, *exchange(*faces), *tables, sums_1

time: 74.7 us -> 69.9 us (0.936)
  starting transfers between devices: 20.6 us -> 14.2 us
  Pallas kernels: 20.5 us -> 16.8 us
  local copies, waits for them, and re-layouts: 6.93 us -> 9.33 us
  other arithmetic: 2.79 us -> 4.51 us
    ppermute x14 -> x10, starting transfers between devices: 20.6 us -> 14.2 us  [shifted(): return lax.ppermute(value, axis, pairs)]
    pallas_call x5, Pallas kernels: 20.5 us -> 16.8 us  [call(): pl.pallas_call(kernel, out_shape=[jax.ShapeDtypeStruct(shape, jnp.float32...]
    slice x6 -> x10, local copies, waits for them, and re-layouts: 0.95 us -> 4.2 us  [the longest x4 1.51 us: face_corners(): return jnp.concatenate([first, face[:, 1:-1], last], axis=1)]
    reshape x1, other arithmetic: 0.74 us -> 1.71 us  [body(): right = (jnp.asarray(stiff_part, jnp.float32) / tall + jnp.asarray(mass_p...]
    squeeze x1 -> x0, local copies, waits for them, and re-layouts: 0.96 us -> none  [packed_near(): block = velocity_old[comp, ex * 8:ex * 8 + 8]]
    ppermute x14 -> x10, waiting for transfers between devices: 11.5 us -> 12.2 us  [shifted(): return lax.ppermute(value, axis, pairs)]
    unnamed x48 -> x34, local copies, waits for them, and re-layouts: 4.48 us -> 4.51 us
  transfers between devices with their start and end apart: 14 -> 10, of which waited for: 6 -> 6; matrix products, arithmetic and copies ran while one was open for 5% -> 7% of each run, Pallas kernels for 7% -> 0%
where the time goes in v3:
time: 69.9 us; the launch traced here: 69 us
  Pallas kernels  16.8 us (24%)
  starting transfers between devices  14.2 us (20%)
  waiting for transfers between devices  12.2 us (17%)
  blocking collectives  10.4 us (15%)
  local copies, waits for them, and re-layouts  9.33 us (13%)
  other arithmetic  4.51 us (6%)
  between operations  0.85 us (1%)
  matrix products  0.71 us (1%)
    pallas_call x5, Pallas kernels, call(): pl.pallas_call(kernel, out_shape=[jax.ShapeDtypeStruct(shape, jnp.float32...  16.8 us
    ppermute x10, starting transfers between devices, shifted(): return lax.ppermute(value, axis, pairs)  14.2 us
    ppermute x10, waiting for transfers between devices, shifted(): return lax.ppermute(value, axis, pairs)  12.2 us
    all_to_all x1, blocking collectives, body(): moments = lax.all_to_all(moments, ('wall', 'span'), 0, 0, tiled=True)  10.4 us
    unnamed x34, local copies, waits for them, and re-layouts  4.51 us
    reshape x1, other arithmetic, body(): right = (jnp.asarray(stiff_part, jnp.float32) / tall + jnp.asarray(mass_p...  1.71 us
    slice x4, local copies, waits for them, and re-layouts, face_corners(): return jnp.concatenate([first, face[:, 1:-1], last], axis=1)  1.51 us
    add x2, other arithmetic, face_corners(): first = face[:, :1] + from_prev[:, spot]  1.48 us
  transfers between devices with their start and end apart: 10, of which 6 were waited for; matrix products, arithmetic and copies ran while one was open for 7% of the time, Pallas kernels for 0%

profile of v3, /device:TPU:0, one launch (start us, length us, event | category | flops | bytes accessed | tf_op | source)
XLA Modules:
  0.0 69.0 jit_solution(1450640152182059048)
XLA Ops:
  0.6 1.7 %fusion.right_ref = f32[128,256]{1,0:T(8,128)} fusion(f32[16,8,256]{2,1,0:T(8,128)} %constant.66.clone, f32[16,8,256]{2,1,0:T(8,128)} %constant.67.clone, f32[16]{0:T(128)} %param.15), kind=kLoop, calls=%fused_computation.3 | loop fusion | flops 98304 | bytes 393280 | tf_op jit(solution)/shard_map/reshape | solution.py:158
  2.3 3.7 %shard_map.149 = (f32[3,16,16,128]{3,2,1,0:T(8,128)}, f32[176,128]{1,0:T(8,128)}, f32[176,128]{1,0:T(8,128)}, f32[3,16,128]{2,1,0:T(8,128)}, f32[3,16,128]{2,1,0:T(8,128)}) custom-call(f32[3,16,16,128]{3,2,1,0:T(8,128)} %v.3, f32[128,256]{1,0:T(8,128)} %constant.65.clone.left_ref, f32[128,256]{1,0:T(8,128)} %fusion.right_ref, f32[256,8]{1,0:T(8,128)} %constant.68.clone.cols), custom_call_target="tpu_custom_call" | custom-call | tf_op jit(solution)/shard_map/pallas_call | solution.py:104
  6.5 2.9 %collective-permute-start.1 = (f32[176,128]{1,0:T(8,128)}, f32[176,128]{1,0:T(8,128)S(1)}, u32[]{:S(2)}, u32[]{:S(2)}) collective-permute-start(f32[176,128]{1,0:T(8,128)} %get-tuple-element.19.own), channel_id=1, source_target_pairs={{0,28},{4,0},{8,4},{12,8},{16,12},{20,16},{24,20},{28,24},{1,29},{... | collective-permute-start | bytes 270344 | tf_op jit(solution)/shard_map/ppermute | solution.py:45
  9.4 0.7 copy-done.14
  10.1 0.7 %slice.93 = f32[3,14,128]{2,1,0:T(8,128)S(1)} slice(f32[3,16,128]{2,1,0:T(8,128)} %get-tuple-element.22), slice={[0:3], [1:15], [0:128]} | slice | bytes 43008 | tf_op jit(solution)/shard_map/slice | solution.py:91
  10.9 0.6 copy-done.15
  11.6 0.6 pad_maximum_fusion.6.info
  12.2 0.6 copy-done
  12.8 0.6 copy-done.1
  13.5 3.0 %shard_map.150 = (f32[2,512]{1,0:T(2,128)}, f32[4,256]{1,0:T(4,128)}) custom-call(f32[176,128]{1,0:T(8,128)} %get-tuple-element.19.own, f32[176,128]{1,0:T(8,128)} %copy-done, f32[176,128]{1,0:T(8,128)} %copy-done.1, f32[6,512]{1,0:T(8,128)} %pad_maximum_fusion.6.info, f32[1,256]{1,0:T(1,128)} %constant.70.clone.mass), custom_call_target="tpu_custom_call" | custom-call | tf_op jit(solution)/shard_map/pallas_call | solution.py:104
  16.5 1.6 %collective-permute-start.3 = (f32[4,256]{1,0:T(4,128)}, f32[4,256]{1,0:T(4,128)S(1)}, u32[]{:S(2)}, u32[]{:S(2)}) collective-permute-start(f32[4,256]{1,0:T(4,128)} %get-tuple-element.21), channel_id=1, source_target_pairs={{0,28},{4,0},{8,4},{12,8},{16,12},{20,16},{24,20},{28,24},{1,29},{... | collective-permute-start | bytes 12296 | tf_op jit(solution)/shard_map/ppermute | solution.py:45
  18.2 0.7 %slice.120 = f32[48,128]{1,0:T(8,128)S(1)} slice(f32[176,128]{1,0:T(8,128)} %copy-done), slice={[128:176], [0:128]} | slice | bytes 49152 | tf_op jit(solution)/shard_map/slice | solution.py:431
  18.9 0.7 %slice.122 = f32[48,128]{1,0:T(8,128)S(1)} slice(f32[176,128]{1,0:T(8,128)} %copy-done.1), slice={[128:176], [0:128]} | slice | bytes 49152 | tf_op jit(solution)/shard_map/slice | solution.py:432
  19.6 0.7 %slice_add_fusion.8 = (f32[3,1,128]{2,1,0:T(1,128)S(1)}, f32[3,1,128]{2,1,0:T(1,128)S(1)}, f32[3,1,128]{2,1,0:T(1,128)S(1)}, f32[3,1,128]{2,1,0:T(1,128)S(1)}) fusion(f32[3,16,128]{2,1,0:T(8,128)S(1)} %bitcast.50, f32[3,16,128]{2,1,0:T(8,128)} %get-tuple-element.22, f32[3,16,128]{2,1,0:T(8,128)S(1)} %bitcast.52, f32[3,16,128]{2,1,0:T(8,128)S(1)} %copy-done.6), kind=kLoop, calls=%fused_computation.37 | loop fusion | flops 1536 | bytes 18432 | tf_op jit(solution)/shard_map/add | solution.py:89
  20.4 1.9 %collective-permute-done.2 = f32[4,256]{1,0:T(4,128)S(1)} collective-permute-done((f32[4,256]{1,0:T(4,128)}, f32[4,256]{1,0:T(4,128)S(1)}, u32[]{:S(2)}, u32[]{:S(2)}) %collective-permute-start.2) | collective-permute-done | bytes 4128 | tf_op jit(solution)/shard_map/ppermute | solution.py:45
  22.4 0.6 copy-done.11
  23.4 4.4 %collective-permute-start.5 = (f32[72,128]{1,0:T(8,128)S(1)}, f32[72,128]{1,0:T(8,128)S(1)}, u32[]{:S(2)}, u32[]{:S(2)}) collective-permute-start(f32[72,128]{1,0:T(8,128)S(1)} %get-tuple-element.48), channel_id=1, source_target_pairs={{0,3},{1,0},{2,1},{3,2},{4,7},{5,4},{6,5},{7,6},{8,11},{9,8},{10,9... | collective-permute-start | bytes 110600 | tf_op jit(solution)/shard_map/ppermute | solution.py:45
  27.8 1.6 %collective-permute-done.5 = f32[72,128]{1,0:T(8,128)S(1)} collective-permute-done((f32[72,128]{1,0:T(8,128)S(1)}, f32[72,128]{1,0:T(8,128)S(1)}, u32[]{:S(2)}, u32[]{:S(2)}) %collective-permute-start.5) | collective-permute-done | bytes 36896 | tf_op jit(solution)/shard_map/ppermute | solution.py:45
  29.5 4.0 %collective-permute-done.4 = f32[72,128]{1,0:T(8,128)S(1)} collective-permute-done((f32[72,128]{1,0:T(8,128)S(1)}, f32[72,128]{1,0:T(8,128)S(1)}, u32[]{:S(2)}, u32[]{:S(2)}) %collective-permute-start.4) | collective-permute-done | bytes 36896 | tf_op jit(solution)/shard_map/ppermute | solution.py:45
  33.6 0.6 copy-done.8
  35.0 0.6 pad_maximum_fusion.7.wall_in
  36.8 4.2 %shard_map.151 = (f32[3,16,16,128]{3,2,1,0:T(8,128)}, f32[3,16,16,128]{3,2,1,0:T(8,128)}, f32[3,16,16,128]{3,2,1,0:T(8,128)}, f32[3,16,128]{2,1,0:T(8,128)}, f32...) custom-call(f32[3,16,16,128]{3,2,1,0:T(8,128)} %v.3, ...), custom_call_target="tpu_custom_call" | custom-call | tf_op jit(solution)/shard_map/pallas_call | solution.py:104
  41.1 2.6 %collective-permute-start.7 = (f32[3,16,128]{2,1,0:T(8,128)}, f32[3,16,128]{2,1,0:T(8,128)S(1)}, u32[]{:S(2)}, u32[]{:S(2)}) collective-permute-start(f32[3,16,128]{2,1,0:T(8,128)} %get-tuple-element.27), channel_id=1, source_target_pairs={{0,28},{4,0},{8,4},{12,8},{16,12},{20,16},{24,20},{28,24},{1,29},{... | collective-permute-start | bytes 73736 | tf_op jit(solution)/shard_map/ppermute | solution.py:45
  43.7 0.7 %slice.112 = f32[3,14,128]{2,1,0:T(8,128)S(1)} slice(f32[3,16,128]{2,1,0:T(8,128)} %get-tuple-element.28), slice={[0:3], [1:15], [0:128]} | slice | bytes 43008 | tf_op jit(solution)/shard_map/slice | solution.py:91
  44.5 1.0 %collective-permute-done.6.xp = f32[3,16,128]{2,1,0:T(8,128)S(1)} collective-permute-done((f32[3,16,128]{2,1,0:T(8,128)}, f32[3,16,128]{2,1,0:T(8,128)S(1)}, u32[]{:S(2)}, u32[]{:S(2)}) %collective-permute-start.6) | collective-permute-done | bytes 24608 | tf_op jit(solution)/shard_map/ppermute | solution.py:45
  45.4 0.7 %slice_add_fusion.2 = (f32[3,1,128]{2,1,0:T(1,128)S(1)}, f32[3,1,128]{2,1,0:T(1,128)S(1)}, f32[3,1,128]{2,1,0:T(1,128)S(1)}, f32[3,1,128]{2,1,0:T(1,128)S(1)}) fusion(f32[3,16,128]{2,1,0:T(8,128)S(1)} %collective-permute-done.6.xp, f32[3,16,128]{2,1,0:T(8,128)S(1)} %copy-done.7, f32[3,16,128]{2,1,0:T(8,128)S(1)} %collective-permute-done.7.xn, ...), kind=kLoop, calls=%fused_computation.31 | loop fusion | flops 1536 | bytes 18432 | tf_op jit(solution)/shard_map/add | solution.py:89
  46.4 2.0 %collective-permute-start.8 = (f32[3,16,128]{2,1,0:T(8,128)S(1)}, f32[3,16,128]{2,1,0:T(8,128)S(1)}, u32[]{:S(2)}, u32[]{:S(2)}) collective-permute-start(f32[3,16,128]{2,1,0:T(8,128)S(1)} %pad_maximum_fusion.4), channel_id=1, source_target_pairs={{0,1},{1,2},{2,3},{3,0},{4,5},{5,6},{6,7},{7,4},{8,9},{9,10},{10,1... | collective-permute-start | bytes 73736 | tf_op jit(solution)/shard_map/ppermute | solution.py:45
  48.4 1.7 %collective-permute-done.9.zn = f32[3,16,128]{2,1,0:T(8,128)S(1)} collective-permute-done((f32[3,16,128]{2,1,0:T(8,128)S(1)}, f32[3,16,128]{2,1,0:T(8,128)S(1)}, u32[]{:S(2)}, u32[]{:S(2)}) %collective-permute-start.9) | collective-permute-done | bytes 24608 | tf_op jit(solution)/shard_map/ppermute | solution.py:45
  50.1 2.0 %collective-permute-done.8.zp = f32[3,16,128]{2,1,0:T(8,128)S(1)} collective-permute-done((f32[3,16,128]{2,1,0:T(8,128)S(1)}, f32[3,16,128]{2,1,0:T(8,128)S(1)}, u32[]{:S(2)}, u32[]{:S(2)}) %collective-permute-start.8) | collective-permute-done | bytes 24608 | tf_op jit(solution)/shard_map/ppermute | solution.py:45
  52.7 3.6 %shard_map.152 = (f32[3,16,16,128]{3,2,1,0:T(8,128)}, f32[32,18]{1,0:T(8,128)}) custom-call(f32[3,16,16,128]{3,2,1,0:T(8,128)} %get-tuple-element.25.t_in, f32[3,16,128]{2,1,0:T(8,128)} %copy-done.4, f32[3,16,128]{2,1,0:T(8,128)} %copy-done.5, f32[3,16,128]{2,1,0:T(8,128)} %copy-done.10, f32[3,16,128]{2,1,0:T(8,128)} %copy-done.9, ...), custom_call_target="tpu_custom_call" | custom-call | tf_op jit(solution)/shard_map/pallas_call | solution.py:104
  56.3 10.4 %all_to_all.11 = f32[32,1,18]{2,1,0:T(1,128)} all-to-all(f32[32,1,18]{2,1,0:T(1,128)} %bitcast.59), channel_id=1, replica_groups=mesh['wall'=8,'span'=4] {'wall','span'}, dimensions={0} | all-to-all | bytes 4608 | tf_op jit(solution)/shard_map/all_to_all | solution.py:456
  66.8 2.3 %shard_map.153 = f32[3,16,16,128]{3,2,1,0:T(8,128)} custom-call(f32[32,18]{1,0:T(8,128)} %bitcast.58, f32[3,16,16,128]{3,2,1,0:T(8,128)} %get-tuple-element.32.u0, f32[3,16,16,128]{3,2,1,0:T(8,128)} %get-tuple-element.33.u1, f32[3,16,16,128]{3,2,1,0:T(8,128)} %get-tuple-element.34.u2), custom_call_target="tpu_custom_call" | custom-call | tf_op jit(solution)/shard_map/pallas_call | solution.py:104
  (61 shorter events, 4.0 us)
Async XLA Ops:
  6.0 6.2 %collective-permute-start = (f32[176,128]{1,0:T(8,128)}, f32[176,128]{1,0:T(8,128)S(1)}, u32[]{:S(2)}, u32[]{:S(2)}) collective-permute-start(f32[176,128]{1,0:T(8,128)} %get-tuple-element.20), channel_id=1, source_target_pairs={{0,4},{4,8},{8,12},{12,16},{16,20},{20,24},{24,28},{28,0},{1,5},{5... | collective-permute-start | bytes 270344 | tf_op jit(solution)/shard_map/ppermute | solution.py:45
  6.5 5.7 %collective-permute-start.1 = (f32[176,128]{1,0:T(8,128)}, f32[176,128]{1,0:T(8,128)S(1)}, u32[]{:S(2)}, u32[]{:S(2)}) collective-permute-start(f32[176,128]{1,0:T(8,128)} %get-tuple-element.19.own), channel_id=1, source_target_pairs={{0,28},{4,0},{8,4},{12,8},{16,12},{20,16},{24,20},{28,24},{1,29},{... | collective-permute-start | bytes 270344 | tf_op jit(solution)/shard_map/ppermute | solution.py:45
  9.4 0.7 copy-start.14
  10.1 0.8 %copy-start.6 = (f32[3,16,128]{2,1,0:T(8,128)S(1)}, f32[3,16,128]{2,1,0:T(8,128)}, u32[]{:S(2)}) copy-start(f32[3,16,128]{2,1,0:T(8,128)} %get-tuple-element.23) | copy-start | bytes 73732
  10.9 0.7 copy-start.15
  10.9 0.7 %copy-start.12 = (f32[3,512]{1,0:T(4,128)S(1)}, f32[3,512]{1,0:T(4,128)}, u32[]{:S(2)}) copy-start(f32[3,512]{1,0:T(4,128)} %param.18) | copy-start | bytes 18436
  10.9 0.7 %copy-start.16 = (f32[512]{0:T(512)S(1)}, f32[512]{0:T(512)}, u32[]{:S(2)}) copy-start(f32[512]{0:T(512)} %param.19) | copy-start | bytes 6148
  12.2 0.6 copy-start
  12.8 0.6 copy-start.1
  16.5 3.9 %collective-permute-start.3 = (f32[4,256]{1,0:T(4,128)}, f32[4,256]{1,0:T(4,128)S(1)}, u32[]{:S(2)}, u32[]{:S(2)}) collective-permute-start(f32[4,256]{1,0:T(4,128)} %get-tuple-element.21), channel_id=1, source_target_pairs={{0,28},{4,0},{8,4},{12,8},{16,12},{20,16},{24,20},{28,24},{1,29},{... | collective-permute-start | bytes 12296 | tf_op jit(solution)/shard_map/ppermute | solution.py:45
  18.2 4.1 %collective-permute-start.2 = (f32[4,256]{1,0:T(4,128)}, f32[4,256]{1,0:T(4,128)S(1)}, u32[]{:S(2)}, u32[]{:S(2)}) collective-permute-start(f32[4,256]{1,0:T(4,128)} %get-tuple-element.21), channel_id=1, source_target_pairs={{0,4},{4,8},{8,12},{12,16},{16,20},{20,24},{24,28},{28,0},{1,5},{5... | collective-permute-start | bytes 12296 | tf_op jit(solution)/shard_map/ppermute | solution.py:45
  18.9 0.8 %copy-start.2 = (f32[48,128]{1,0:T(8,128)}, f32[48,128]{1,0:T(8,128)S(1)}, u32[]{:S(2)}) copy-start(f32[48,128]{1,0:T(8,128)S(1)} %slice.120) | copy-start | bytes 73732
  19.6 0.8 %copy-start.3 = (f32[48,128]{1,0:T(8,128)}, f32[48,128]{1,0:T(8,128)S(1)}, u32[]{:S(2)}) copy-start(f32[48,128]{1,0:T(8,128)S(1)} %slice.122) | copy-start | bytes 73732
  20.4 1.9 %copy-start.13 = (f32[4,256]{1,0:T(4,128)S(1)}, f32[4,256]{1,0:T(4,128)}, u32[]{:S(2)}) copy-start(f32[4,256]{1,0:T(4,128)} %get-tuple-element.21) | copy-start | bytes 12292
  22.3 0.7 %copy-start.11 = (f32[3,16,48,1]{2,1,0,3:T(8,128)S(1)}, f32[3,16,48,1]{2,1,0,3:T(8,128)}, u32[]{:S(2)}) copy-start(f32[3,16,48,1]{2,1,0,3:T(8,128)} %constant.73) | copy-start | bytes 27652
  23.4 6.0 %collective-permute-start.5 = (f32[72,128]{1,0:T(8,128)S(1)}, f32[72,128]{1,0:T(8,128)S(1)}, u32[]{:S(2)}, u32[]{:S(2)}) collective-permute-start(f32[72,128]{1,0:T(8,128)S(1)} %get-tuple-element.48), channel_id=1, source_target_pairs={{0,3},{1,0},{2,1},{3,2},{4,7},{5,4},{6,5},{7,6},{8,11},{9,8},{10,9... | collective-permute-start | bytes 110600 | tf_op jit(solution)/shard_map/ppermute | solution.py:45
  27.8 5.8 %collective-permute-start.4 = (f32[72,128]{1,0:T(8,128)S(1)}, f32[72,128]{1,0:T(8,128)S(1)}, u32[]{:S(2)}, u32[]{:S(2)}) collective-permute-start(f32[72,128]{1,0:T(8,128)S(1)} %get-tuple-element.47), channel_id=1, source_target_pairs={{0,1},{1,2},{2,3},{3,0},{4,5},{5,6},{6,7},{7,4},{8,9},{9,10},{10,1... | collective-permute-start | bytes 110600 | tf_op jit(solution)/shard_map/ppermute | solution.py:45
  33.5 0.7 %copy-start.8 = (f32[3,16,48,1,1]{2,1,0,4,3:T(8,128)S(1)}, f32[3,16,48,1,1]{2,1,0,4,3:T(8,128)}, u32[]{:S(2)}) copy-start(f32[3,16,48,1,1]{2,1,0,4,3:T(8,128)} %constant.74) | copy-start | bytes 27652
  41.0 4.4 %collective-permute-start.6 = (f32[3,16,128]{2,1,0:T(8,128)}, f32[3,16,128]{2,1,0:T(8,128)S(1)}, u32[]{:S(2)}, u32[]{:S(2)}) collective-permute-start(f32[3,16,128]{2,1,0:T(8,128)} %get-tuple-element.26), channel_id=1, source_target_pairs={{0,4},{4,8},{8,12},{12,16},{16,20},{20,24},{24,28},{28,0},{1,5},{5... | collective-permute-start | bytes 73736 | tf_op jit(solution)/shard_map/ppermute | solution.py:45
  41.1 4.4 %collective-permute-start.7 = (f32[3,16,128]{2,1,0:T(8,128)}, f32[3,16,128]{2,1,0:T(8,128)S(1)}, u32[]{:S(2)}, u32[]{:S(2)}) collective-permute-start(f32[3,16,128]{2,1,0:T(8,128)} %get-tuple-element.27), channel_id=1, source_target_pairs={{0,28},{4,0},{8,4},{12,8},{16,12},{20,16},{24,20},{28,24},{1,29},{... | collective-permute-start | bytes 73736 | tf_op jit(solution)/shard_map/ppermute | solution.py:45
  43.7 0.8 %copy-start.7 = (f32[3,16,128]{2,1,0:T(8,128)S(1)}, f32[3,16,128]{2,1,0:T(8,128)}, u32[]{:S(2)}) copy-start(f32[3,16,128]{2,1,0:T(8,128)} %get-tuple-element.29) | copy-start | bytes 73732
  45.4 0.8 %copy-start.4 = (f32[3,16,128]{2,1,0:T(8,128)}, f32[3,16,128]{2,1,0:T(8,128)S(1)}, u32[]{:S(2)}) copy-start(f32[3,16,128]{2,1,0:T(8,128)S(1)} %collective-permute-done.6.xp) | copy-start | bytes 73732
  45.4 0.8 %copy-start.5 = (f32[3,16,128]{2,1,0:T(8,128)}, f32[3,16,128]{2,1,0:T(8,128)S(1)}, u32[]{:S(2)}) copy-start(f32[3,16,128]{2,1,0:T(8,128)S(1)} %collective-permute-done.7.xn) | copy-start | bytes 73732
  46.2 3.9 %collective-permute-start.9 = (f32[3,16,128]{2,1,0:T(8,128)S(1)}, f32[3,16,128]{2,1,0:T(8,128)S(1)}, u32[]{:S(2)}, u32[]{:S(2)}) collective-permute-start(f32[3,16,128]{2,1,0:T(8,128)S(1)} %pad_maximum_fusion.5), channel_id=1, source_target_pairs={{0,3},{1,0},{2,1},{3,2},{4,7},{5,4},{6,5},{7,6},{8,11},{9,8},{10,9... | collective-permute-start | bytes 73736 | tf_op jit(solution)/shard_map/ppermute | solution.py:45
  46.4 5.7 %collective-permute-start.8 = (f32[3,16,128]{2,1,0:T(8,128)S(1)}, f32[3,16,128]{2,1,0:T(8,128)S(1)}, u32[]{:S(2)}, u32[]{:S(2)}) collective-permute-start(f32[3,16,128]{2,1,0:T(8,128)S(1)} %pad_maximum_fusion.4), channel_id=1, source_target_pairs={{0,1},{1,2},{2,3},{3,0},{4,5},{5,6},{6,7},{7,4},{8,9},{9,10},{10,1... | collective-permute-start | bytes 73736 | tf_op jit(solution)/shard_map/ppermute | solution.py:45
  50.1 2.0 %copy-start.9 = (f32[3,16,128]{2,1,0:T(8,128)}, f32[3,16,128]{2,1,0:T(8,128)S(1)}, u32[]{:S(2)}) copy-start(f32[3,16,128]{2,1,0:T(8,128)S(1)} %collective-permute-done.9.zn) | copy-start | bytes 73732
  52.1 0.6 copy-start.10

commit v4 on v3

--- a/solution.py
+++ b/solution.py
@@ -320,6 +320,14 @@
         lane = lax.broadcasted_iota(jnp.int32, (plane, length_y), 1)
         sums[...] = jnp.zeros((16, length_y), jnp.float32)
         fields = []
+        xp, xn = (
+            [m[slab + c * length_z : slab + (c + 1) * length_z, :] for c in range(3)]
+            for m in (xp, xn)
+        )
+        zp, zn = (
+            [m[size + c * length_x : size + (c + 1) * length_x, :] for c in range(3)]
+            for m in (zp, zn)
+        )
         for comp in range(3):
             base = smooth_part(comp, v, cols, right_ref)
             field = add_faces(comp, t_in, xp, xn, zp, zn)
@@ -440,7 +448,7 @@
     wide = jnp.concatenate(
         [z_prev[:size].reshape(along.shape), along, z_next[:size].reshape(along.shape)], axis=3
     )
-    around = (x_prev, x_next, z_prev[size:].reshape(z_face), z_next[size:].reshape(z_face))
+    around = (from_prev, from_next, z_prev, z_next)
     both = jnp.einsum("ocxs,pzs->opcxz", wide, ops_z, precision=precise)
     walls = jnp.concatenate(
         [both[0, 0], both[1, 1], viscosity * (both[2, 1] + both[1, 2])], axis=0

time: 69.9 us -> 69.2 us (0.990)
  local copies, waits for them, and re-layouts: 9.33 us -> 7.89 us
  waiting for transfers between devices: 12.2 us -> 12.9 us
    slice x2 -> x0, local copies, waits for them, and re-layouts: 1.2 us -> none  [the longest x1 0.6 us: body(): z_prev[size:].reshape(z_face)]
    ppermute x10, waiting for transfers between devices: 12.2 us -> 12.9 us  [shifted(): return lax.ppermute(value, axis, pairs)]
    slice x1 -> x2, local copies, waits for them, and re-layouts: 0.75 us -> 0.02 us  [body(): x_next = from_next[slab:].reshape(x_face)]
  transfers between devices with their start and end apart: 10 -> 10, of which waited for: 6 -> 6; matrix products, arithmetic and copies ran while one was open for 7% -> 4% of each run, Pallas kernels for 0% -> 0%
where the time goes in v4:
time: 69.2 us; the launch traced here: 68.4 us
  Pallas kernels  16.9 us (24%)
  starting transfers between devices  14.3 us (21%)
  waiting for transfers between devices  12.9 us (19%)
  blocking collectives  10.4 us (15%)
  local copies, waits for them, and re-layouts  7.89 us (11%)
  other arithmetic  4.49 us (6%)
  between operations  0.84 us (1%)
  matrix products  0.71 us (1%)
    pallas_call x5, Pallas kernels, call(): pl.pallas_call(kernel, out_shape=[jax.ShapeDtypeStruct(shape, jnp.float32...  16.9 us
    ppermute x10, starting transfers between devices, shifted(): return lax.ppermute(value, axis, pairs)  14.3 us
    ppermute x10, waiting for transfers between devices, shifted(): return lax.ppermute(value, axis, pairs)  12.9 us
    all_to_all x1, blocking collectives, body(): moments = lax.all_to_all(moments, ('wall', 'span'), 0, 0, tiled=True)  10.4 us
    unnamed x34, local copies, waits for them, and re-layouts  5.01 us
    reshape x1, other arithmetic, body(): right = (jnp.asarray(stiff_part, jnp.float32) / tall + jnp.asarray(mass_p...  1.71 us
    slice x4, local copies, waits for them, and re-layouts, face_corners(): return jnp.concatenate([first, face[:, 1:-1], last], axis=1)  1.51 us
    add x2, other arithmetic, face_corners(): first = face[:, :1] + from_prev[:, spot]  1.47 us
  transfers between devices with their start and end apart: 10, of which 6 were waited for; matrix products, arithmetic and copies ran while one was open for 4% of the time, Pallas kernels for 0%

profile of v4, /device:TPU:0, one launch (start us, length us, event | category | flops | bytes accessed | tf_op | source)
XLA Modules:
  0.0 68.4 jit_solution(10244796670546365861)
XLA Ops:
  0.6 1.7 %fusion.right_ref = f32[128,256]{1,0:T(8,128)} fusion(f32[16,8,256]{2,1,0:T(8,128)} %constant.66.clone, f32[16,8,256]{2,1,0:T(8,128)} %constant.67.clone, f32[16]{0:T(128)} %param.15), kind=kLoop, calls=%fused_computation.3 | loop fusion | flops 98304 | bytes 393280 | tf_op jit(solution)/shard_map/reshape | solution.py:158
  2.3 3.7 %shard_map.149 = (f32[3,16,16,128]{3,2,1,0:T(8,128)}, f32[176,128]{1,0:T(8,128)}, f32[176,128]{1,0:T(8,128)}, f32[3,16,128]{2,1,0:T(8,128)}, f32[3,16,128]{2,1,0:T(8,128)}) custom-call(f32[3,16,16,128]{3,2,1,0:T(8,128)} %v.3, f32[128,256]{1,0:T(8,128)} %constant.65.clone.left_ref, f32[128,256]{1,0:T(8,128)} %fusion.right_ref, f32[256,8]{1,0:T(8,128)} %constant.68.clone.cols), custom_call_target="tpu_custom_call" | custom-call | tf_op jit(solution)/shard_map/pallas_call | solution.py:104
  6.5 2.9 %collective-permute-start.1 = (f32[176,128]{1,0:T(8,128)}, f32[176,128]{1,0:T(8,128)S(1)}, u32[]{:S(2)}, u32[]{:S(2)}) collective-permute-start(f32[176,128]{1,0:T(8,128)} %get-tuple-element.19.own), channel_id=1, source_target_pairs={{0,28},{4,0},{8,4},{12,8},{16,12},{20,16},{24,20},{28,24},{1,29},{... | collective-permute-start | bytes 270344 | tf_op jit(solution)/shard_map/ppermute | solution.py:45
  9.4 0.7 copy-done.14
  10.1 0.7 %slice.87 = f32[3,14,128]{2,1,0:T(8,128)S(1)} slice(f32[3,16,128]{2,1,0:T(8,128)} %get-tuple-element.22), slice={[0:3], [1:15], [0:128]} | slice | bytes 43008 | tf_op jit(solution)/shard_map/slice | solution.py:91
  10.9 0.6 copy-done.15
  11.6 0.6 pad_maximum_fusion.6.info
  12.2 0.6 copy-done
  12.8 0.6 copy-done.1
  13.5 3.0 %shard_map.150 = (f32[2,512]{1,0:T(2,128)}, f32[4,256]{1,0:T(4,128)}) custom-call(f32[176,128]{1,0:T(8,128)} %get-tuple-element.19.own, f32[176,128]{1,0:T(8,128)} %copy-done, f32[176,128]{1,0:T(8,128)} %copy-done.1, f32[6,512]{1,0:T(8,128)} %pad_maximum_fusion.6.info, f32[1,256]{1,0:T(1,128)} %constant.70.clone.mass), custom_call_target="tpu_custom_call" | custom-call | tf_op jit(solution)/shard_map/pallas_call | solution.py:104
  16.5 1.7 %collective-permute-start.3 = (f32[4,256]{1,0:T(4,128)}, f32[4,256]{1,0:T(4,128)S(1)}, u32[]{:S(2)}, u32[]{:S(2)}) collective-permute-start(f32[4,256]{1,0:T(4,128)} %get-tuple-element.21), channel_id=1, source_target_pairs={{0,28},{4,0},{8,4},{12,8},{16,12},{20,16},{24,20},{28,24},{1,29},{... | collective-permute-start | bytes 12296 | tf_op jit(solution)/shard_map/ppermute | solution.py:45
  18.2 0.7 %slice-done = f32[48,128]{1,0:T(8,128)S(1)} async-done(((f32[176,128]{1,0:T(8,128)}), f32[48,128]{1,0:T(8,128)S(1)}, s32[]{:S(2)}) %slice-start) | async-done | bytes 24600 | tf_op jit(solution)/shard_map/slice | solution.py:439
  18.9 0.7 %slice_add_fusion.8 = (f32[3,1,128]{2,1,0:T(1,128)S(1)}, f32[3,1,128]{2,1,0:T(1,128)S(1)}, f32[3,1,128]{2,1,0:T(1,128)S(1)}, f32[3,1,128]{2,1,0:T(1,128)S(1)}) fusion(f32[3,16,128]{2,1,0:T(8,128)S(1)} %bitcast.48, f32[3,16,128]{2,1,0:T(8,128)} %get-tuple-element.22, f32[3,16,128]{2,1,0:T(8,128)S(1)} %bitcast.49, f32[3,16,128]{2,1,0:T(8,128)S(1)} %copy-done.6), kind=kLoop, calls=%fused_computation.37 | loop fusion | flops 1536 | bytes 18432 | tf_op jit(solution)/shard_map/add | solution.py:89
  19.7 2.6 %collective-permute-done.2 = f32[4,256]{1,0:T(4,128)S(1)} collective-permute-done((f32[4,256]{1,0:T(4,128)}, f32[4,256]{1,0:T(4,128)S(1)}, u32[]{:S(2)}, u32[]{:S(2)}) %collective-permute-start.2) | collective-permute-done | bytes 4128 | tf_op jit(solution)/shard_map/ppermute | solution.py:45
  22.4 0.6 copy-done.11
  23.4 4.4 %collective-permute-start.5 = (f32[72,128]{1,0:T(8,128)S(1)}, f32[72,128]{1,0:T(8,128)S(1)}, u32[]{:S(2)}, u32[]{:S(2)}) collective-permute-start(f32[72,128]{1,0:T(8,128)S(1)} %get-tuple-element.48), channel_id=1, source_target_pairs={{0,3},{1,0},{2,1},{3,2},{4,7},{5,4},{6,5},{7,6},{8,11},{9,8},{10,9... | collective-permute-start | bytes 110600 | tf_op jit(solution)/shard_map/ppermute | solution.py:45
  27.8 1.6 %collective-permute-done.5.zn = f32[72,128]{1,0:T(8,128)S(1)} collective-permute-done((f32[72,128]{1,0:T(8,128)S(1)}, f32[72,128]{1,0:T(8,128)S(1)}, u32[]{:S(2)}, u32[]{:S(2)}) %collective-permute-start.5) | collective-permute-done | bytes 36896 | tf_op jit(solution)/shard_map/ppermute | solution.py:45
  30.0 3.5 %collective-permute-done.4.zp = f32[72,128]{1,0:T(8,128)S(1)} collective-permute-done((f32[72,128]{1,0:T(8,128)S(1)}, f32[72,128]{1,0:T(8,128)S(1)}, u32[]{:S(2)}, u32[]{:S(2)}) %collective-permute-start.4) | collective-permute-done | bytes 36896 | tf_op jit(solution)/shard_map/ppermute | solution.py:45
  35.1 0.6 pad_maximum_fusion.7.wall_in
  35.7 4.2 %shard_map.151 = (f32[3,16,16,128]{3,2,1,0:T(8,128)}, f32[3,16,16,128]{3,2,1,0:T(8,128)}, f32[3,16,16,128]{3,2,1,0:T(8,128)}, f32[3,16,128]{2,1,0:T(8,128)}, f32...) custom-call(f32[3,16,16,128]{3,2,1,0:T(8,128)} %v.3, ...), custom_call_target="tpu_custom_call" | custom-call | tf_op jit(solution)/shard_map/pallas_call | solution.py:104
  40.0 2.6 %collective-permute-start.7 = (f32[3,16,128]{2,1,0:T(8,128)}, f32[3,16,128]{2,1,0:T(8,128)S(1)}, u32[]{:S(2)}, u32[]{:S(2)}) collective-permute-start(f32[3,16,128]{2,1,0:T(8,128)} %get-tuple-element.27), channel_id=1, source_target_pairs={{0,28},{4,0},{8,4},{12,8},{16,12},{20,16},{24,20},{28,24},{1,29},{... | collective-permute-start | bytes 73736 | tf_op jit(solution)/shard_map/ppermute | solution.py:45
  42.6 0.7 %slice.104 = f32[3,14,128]{2,1,0:T(8,128)S(1)} slice(f32[3,16,128]{2,1,0:T(8,128)} %get-tuple-element.28), slice={[0:3], [1:15], [0:128]} | slice | bytes 43008 | tf_op jit(solution)/shard_map/slice | solution.py:91
  43.4 1.0 %collective-permute-done.6.xp = f32[3,16,128]{2,1,0:T(8,128)S(1)} collective-permute-done((f32[3,16,128]{2,1,0:T(8,128)}, f32[3,16,128]{2,1,0:T(8,128)S(1)}, u32[]{:S(2)}, u32[]{:S(2)}) %collective-permute-start.6) | collective-permute-done | bytes 24608 | tf_op jit(solution)/shard_map/ppermute | solution.py:45
  44.4 0.7 %slice_add_fusion.2 = (f32[3,1,128]{2,1,0:T(1,128)S(1)}, f32[3,1,128]{2,1,0:T(1,128)S(1)}, f32[3,1,128]{2,1,0:T(1,128)S(1)}, f32[3,1,128]{2,1,0:T(1,128)S(1)}) fusion(f32[3,16,128]{2,1,0:T(8,128)S(1)} %collective-permute-done.6.xp, f32[3,16,128]{2,1,0:T(8,128)S(1)} %copy-done.7, f32[3,16,128]{2,1,0:T(8,128)S(1)} %collective-permute-done.7.xn, ...), kind=kLoop, calls=%fused_computation.31 | loop fusion | flops 1536 | bytes 18432 | tf_op jit(solution)/shard_map/add | solution.py:89
  45.1 0.7 collective-permute-start.9
  45.8 1.5 %collective-permute-start.8 = (f32[3,16,128]{2,1,0:T(8,128)S(1)}, f32[3,16,128]{2,1,0:T(8,128)S(1)}, u32[]{:S(2)}, u32[]{:S(2)}) collective-permute-start(f32[3,16,128]{2,1,0:T(8,128)S(1)} %pad_maximum_fusion.4), channel_id=1, source_target_pairs={{0,1},{1,2},{2,3},{3,0},{4,5},{5,6},{6,7},{7,4},{8,9},{9,10},{10,1... | collective-permute-start | bytes 73736 | tf_op jit(solution)/shard_map/ppermute | solution.py:45
  47.3 1.7 %collective-permute-done.9.zn = f32[3,16,128]{2,1,0:T(8,128)S(1)} collective-permute-done((f32[3,16,128]{2,1,0:T(8,128)S(1)}, f32[3,16,128]{2,1,0:T(8,128)S(1)}, u32[]{:S(2)}, u32[]{:S(2)}) %collective-permute-start.9) | collective-permute-done | bytes 24608 | tf_op jit(solution)/shard_map/ppermute | solution.py:45
  49.0 2.5 %collective-permute-done.8.zp = f32[3,16,128]{2,1,0:T(8,128)S(1)} collective-permute-done((f32[3,16,128]{2,1,0:T(8,128)S(1)}, f32[3,16,128]{2,1,0:T(8,128)S(1)}, u32[]{:S(2)}, u32[]{:S(2)}) %collective-permute-start.8) | collective-permute-done | bytes 24608 | tf_op jit(solution)/shard_map/ppermute | solution.py:45
  51.5 0.6 copy-done.10
  52.1 3.6 %shard_map.152 = (f32[3,16,16,128]{3,2,1,0:T(8,128)}, f32[32,18]{1,0:T(8,128)}) custom-call(f32[3,16,16,128]{3,2,1,0:T(8,128)} %get-tuple-element.25.t_in, f32[3,16,128]{2,1,0:T(8,128)} %copy-done.4, f32[3,16,128]{2,1,0:T(8,128)} %copy-done.5, f32[3,16,128]{2,1,0:T(8,128)} %copy-done.10, f32[3,16,128]{2,1,0:T(8,128)} %copy-done.9, ...), custom_call_target="tpu_custom_call" | custom-call | tf_op jit(solution)/shard_map/pallas_call | solution.py:104
  55.7 10.4 %all_to_all.11 = f32[32,1,18]{2,1,0:T(1,128)} all-to-all(f32[32,1,18]{2,1,0:T(1,128)} %bitcast.53), channel_id=1, replica_groups=mesh['wall'=8,'span'=4] {'wall','span'}, dimensions={0} | all-to-all | bytes 4608 | tf_op jit(solution)/shard_map/all_to_all | solution.py:464
  66.1 2.3 %shard_map.153 = f32[3,16,16,128]{3,2,1,0:T(8,128)} custom-call(f32[32,18]{1,0:T(8,128)} %bitcast.52, f32[3,16,16,128]{3,2,1,0:T(8,128)} %get-tuple-element.32.u0, f32[3,16,16,128]{3,2,1,0:T(8,128)} %get-tuple-element.33.u1, f32[3,16,16,128]{3,2,1,0:T(8,128)} %get-tuple-element.34.u2), custom_call_target="tpu_custom_call" | custom-call | tf_op jit(solution)/shard_map/pallas_call | solution.py:104
  (61 shorter events, 3.3 us)
Async XLA Ops:
  6.0 6.2 %collective-permute-start = (f32[176,128]{1,0:T(8,128)}, f32[176,128]{1,0:T(8,128)S(1)}, u32[]{:S(2)}, u32[]{:S(2)}) collective-permute-start(f32[176,128]{1,0:T(8,128)} %get-tuple-element.20), channel_id=1, source_target_pairs={{0,4},{4,8},{8,12},{12,16},{16,20},{20,24},{24,28},{28,0},{1,5},{5... | collective-permute-start | bytes 270344 | tf_op jit(solution)/shard_map/ppermute | solution.py:45
  6.5 5.7 %collective-permute-start.1 = (f32[176,128]{1,0:T(8,128)}, f32[176,128]{1,0:T(8,128)S(1)}, u32[]{:S(2)}, u32[]{:S(2)}) collective-permute-start(f32[176,128]{1,0:T(8,128)} %get-tuple-element.19.own), channel_id=1, source_target_pairs={{0,28},{4,0},{8,4},{12,8},{16,12},{20,16},{24,20},{28,24},{1,29},{... | collective-permute-start | bytes 270344 | tf_op jit(solution)/shard_map/ppermute | solution.py:45
  9.4 0.7 copy-start.14
  10.1 0.8 %copy-start.6 = (f32[3,16,128]{2,1,0:T(8,128)S(1)}, f32[3,16,128]{2,1,0:T(8,128)}, u32[]{:S(2)}) copy-start(f32[3,16,128]{2,1,0:T(8,128)} %get-tuple-element.23) | copy-start | bytes 73732
  10.9 0.7 copy-start.15
  10.9 0.7 %copy-start.12 = (f32[3,512]{1,0:T(4,128)S(1)}, f32[3,512]{1,0:T(4,128)}, u32[]{:S(2)}) copy-start(f32[3,512]{1,0:T(4,128)} %param.18) | copy-start | bytes 18436
  10.9 0.7 %copy-start.16 = (f32[512]{0:T(512)S(1)}, f32[512]{0:T(512)}, u32[]{:S(2)}) copy-start(f32[512]{0:T(512)} %param.19) | copy-start | bytes 6148
  12.2 0.6 copy-start
  12.8 0.6 copy-start.1
  16.5 3.2 %collective-permute-start.3 = (f32[4,256]{1,0:T(4,128)}, f32[4,256]{1,0:T(4,128)S(1)}, u32[]{:S(2)}, u32[]{:S(2)}) collective-permute-start(f32[4,256]{1,0:T(4,128)} %get-tuple-element.21), channel_id=1, source_target_pairs={{0,28},{4,0},{8,4},{12,8},{16,12},{20,16},{24,20},{28,24},{1,29},{... | collective-permute-start | bytes 12296 | tf_op jit(solution)/shard_map/ppermute | solution.py:45
  18.2 4.1 %collective-permute-start.2 = (f32[4,256]{1,0:T(4,128)}, f32[4,256]{1,0:T(4,128)S(1)}, u32[]{:S(2)}, u32[]{:S(2)}) collective-permute-start(f32[4,256]{1,0:T(4,128)} %get-tuple-element.21), channel_id=1, source_target_pairs={{0,4},{4,8},{8,12},{12,16},{16,20},{20,24},{24,28},{28,0},{1,5},{5... | collective-permute-start | bytes 12296 | tf_op jit(solution)/shard_map/ppermute | solution.py:45
  18.2 0.7 %slice-start = ((f32[176,128]{1,0:T(8,128)}), f32[48,128]{1,0:T(8,128)S(1)}, s32[]{:S(2)}) async-start(f32[176,128]{1,0:T(8,128)} %copy-done), calls=%async_computation.1 | async-start | bytes 49152 | tf_op jit(solution)/shard_map/slice | solution.py:439
  18.2 0.8 %slice-start.1 = ((f32[176,128]{1,0:T(8,128)}), f32[48,128]{1,0:T(8,128)S(1)}, s32[]{:S(2)}) async-start(f32[176,128]{1,0:T(8,128)} %copy-done.1), calls=%async_computation.2 | async-start | bytes 49152 | tf_op jit(solution)/shard_map/slice | solution.py:440
  19.7 2.7 %copy-start.13 = (f32[4,256]{1,0:T(4,128)S(1)}, f32[4,256]{1,0:T(4,128)}, u32[]{:S(2)}) copy-start(f32[4,256]{1,0:T(4,128)} %get-tuple-element.21) | copy-start | bytes 12292
  22.3 0.7 %copy-start.11 = (f32[3,16,48,1]{2,1,0,3:T(8,128)S(1)}, f32[3,16,48,1]{2,1,0,3:T(8,128)}, u32[]{:S(2)}) copy-start(f32[3,16,48,1]{2,1,0,3:T(8,128)} %constant.73) | copy-start | bytes 27652
  23.4 6.0 %collective-permute-start.5 = (f32[72,128]{1,0:T(8,128)S(1)}, f32[72,128]{1,0:T(8,128)S(1)}, u32[]{:S(2)}, u32[]{:S(2)}) collective-permute-start(f32[72,128]{1,0:T(8,128)S(1)} %get-tuple-element.48), channel_id=1, source_target_pairs={{0,3},{1,0},{2,1},{3,2},{4,7},{5,4},{6,5},{7,6},{8,11},{9,8},{10,9... | collective-permute-start | bytes 110600 | tf_op jit(solution)/shard_map/ppermute | solution.py:45
  27.8 5.8 %collective-permute-start.4 = (f32[72,128]{1,0:T(8,128)S(1)}, f32[72,128]{1,0:T(8,128)S(1)}, u32[]{:S(2)}, u32[]{:S(2)}) collective-permute-start(f32[72,128]{1,0:T(8,128)S(1)} %get-tuple-element.47), channel_id=1, source_target_pairs={{0,1},{1,2},{2,3},{3,0},{4,5},{5,6},{6,7},{7,4},{8,9},{9,10},{10,1... | collective-permute-start | bytes 110600 | tf_op jit(solution)/shard_map/ppermute | solution.py:45
  29.4 0.6 copy-start.2
  33.5 0.6 copy-start.3
  33.6 0.8 %copy-start.8 = (f32[3,16,48,1,1]{2,1,0,4,3:T(8,128)S(1)}, f32[3,16,48,1,1]{2,1,0,4,3:T(8,128)}, u32[]{:S(2)}) copy-start(f32[3,16,48,1,1]{2,1,0,4,3:T(8,128)} %constant.74) | copy-start | bytes 27652
  39.9 4.4 %collective-permute-start.6 = (f32[3,16,128]{2,1,0:T(8,128)}, f32[3,16,128]{2,1,0:T(8,128)S(1)}, u32[]{:S(2)}, u32[]{:S(2)}) collective-permute-start(f32[3,16,128]{2,1,0:T(8,128)} %get-tuple-element.26), channel_id=1, source_target_pairs={{0,4},{4,8},{8,12},{12,16},{16,20},{20,24},{24,28},{28,0},{1,5},{5... | collective-permute-start | bytes 73736 | tf_op jit(solution)/shard_map/ppermute | solution.py:45
  40.0 4.4 %collective-permute-start.7 = (f32[3,16,128]{2,1,0:T(8,128)}, f32[3,16,128]{2,1,0:T(8,128)S(1)}, u32[]{:S(2)}, u32[]{:S(2)}) collective-permute-start(f32[3,16,128]{2,1,0:T(8,128)} %get-tuple-element.27), channel_id=1, source_target_pairs={{0,28},{4,0},{8,4},{12,8},{16,12},{20,16},{24,20},{28,24},{1,29},{... | collective-permute-start | bytes 73736 | tf_op jit(solution)/shard_map/ppermute | solution.py:45
  42.6 0.8 %copy-start.7 = (f32[3,16,128]{2,1,0:T(8,128)S(1)}, f32[3,16,128]{2,1,0:T(8,128)}, u32[]{:S(2)}) copy-start(f32[3,16,128]{2,1,0:T(8,128)} %get-tuple-element.29) | copy-start | bytes 73732
  44.3 0.8 %copy-start.4 = (f32[3,16,128]{2,1,0:T(8,128)}, f32[3,16,128]{2,1,0:T(8,128)S(1)}, u32[]{:S(2)}) copy-start(f32[3,16,128]{2,1,0:T(8,128)S(1)} %collective-permute-done.6.xp) | copy-start | bytes 73732
  44.3 0.8 %copy-start.5 = (f32[3,16,128]{2,1,0:T(8,128)}, f32[3,16,128]{2,1,0:T(8,128)S(1)}, u32[]{:S(2)}) copy-start(f32[3,16,128]{2,1,0:T(8,128)S(1)} %collective-permute-done.7.xn) | copy-start | bytes 73732
  45.1 3.9 %collective-permute-start.9 = (f32[3,16,128]{2,1,0:T(8,128)S(1)}, f32[3,16,128]{2,1,0:T(8,128)S(1)}, u32[]{:S(2)}, u32[]{:S(2)}) collective-permute-start(f32[3,16,128]{2,1,0:T(8,128)S(1)} %pad_maximum_fusion.5), channel_id=1, source_target_pairs={{0,3},{1,0},{2,1},{3,2},{4,7},{5,4},{6,5},{7,6},{8,11},{9,8},{10,9... | collective-permute-start | bytes 73736 | tf_op jit(solution)/shard_map/ppermute | solution.py:45
  45.8 5.7 %collective-permute-start.8 = (f32[3,16,128]{2,1,0:T(8,128)S(1)}, f32[3,16,128]{2,1,0:T(8,128)S(1)}, u32[]{:S(2)}, u32[]{:S(2)}) collective-permute-start(f32[3,16,128]{2,1,0:T(8,128)S(1)} %pad_maximum_fusion.4), channel_id=1, source_target_pairs={{0,1},{1,2},{2,3},{3,0},{4,5},{5,6},{6,7},{7,4},{8,9},{9,10},{10,1... | collective-permute-start | bytes 73736 | tf_op jit(solution)/shard_map/ppermute | solution.py:45
  49.0 2.5 %copy-start.9 = (f32[3,16,128]{2,1,0:T(8,128)}, f32[3,16,128]{2,1,0:T(8,128)S(1)}, u32[]{:S(2)}) copy-start(f32[3,16,128]{2,1,0:T(8,128)S(1)} %collective-permute-done.9.zn) | copy-start | bytes 73732
  51.5 0.6 copy-start.10
